TPU v7x, 32 devices: a whole 2x2x4 slice. The times are simulated.
32 devices in a mesh: rep: 8 (over y, x, core), fsdp: 4 (over z).
Axes of the slice: x: 2, y: 2, z: 4, core: 2. Of those that a mesh axis runs over, the one named last changes fastest.
Arguments:
- block_input: bfloat16 [32, 256, 512], P(('rep', 'fsdp')), may hold values from -6 to 6
- cotangent: bfloat16 [32, 256, 512], P(('rep', 'fsdp')), may hold values from -6 to 6
- seq_valid: int32 [32], P(('rep', 'fsdp')), may hold values 0 or 1
- in_weight: float32 [512, 1536], P('fsdp'), may hold values from -0.25 to 0.25
- out_weight: float32 [512, 512], P('fsdp'), may hold values from -0.75 to 0.75
- small_params: float32 [6914], replicated, may hold values from -8 to 8, as said below
- in_moment: float32 [512, 1536], P('fsdp'), may hold values from -18 to 18
- in_second: float32 [512, 1536], P('fsdp'), may hold values from 1 to 100
- out_moment: float32 [512, 512], P('fsdp'), may hold values from -18 to 18
- out_second: float32 [512, 512], P('fsdp'), may hold values from 1 to 100
- small_moment: float32 [6914], replicated, may hold values from -18 to 18
- small_second: float32 [6914], replicated, may hold values from 1 to 100
Outputs:
- block_output: float32 [32, 256, 512], P(('rep', 'fsdp'))
- input_grad: float32 [32, 256, 512], P(('rep', 'fsdp'))
- in_weight_grad: float32 [512, 1536], P('fsdp')
- out_weight_grad: float32 [512, 512], P('fsdp')
- small_grad: float32 [6914], replicated
- new_in_weight: float32 [512, 1536], P('fsdp')
- new_out_weight: float32 [512, 512], P('fsdp')
- new_small: float32 [6914], replicated
- new_in_moment: float32 [512, 1536], P('fsdp')
- new_in_second: float32 [512, 1536], P('fsdp')
- new_out_moment: float32 [512, 512], P('fsdp')
- new_out_second: float32 [512, 512], P('fsdp')
- new_small_moment: float32 [6914], replicated
- new_small_second: float32 [6914], replicated
Inputs may be any that keep to these rules, and one draw needn't show every extreme that they name: `small_params`: entries 512 + 2 * 2 * 512 + 4 (1024) to that plus 2 lie in -4.7 to 0.
All inputs are finite; a program needn't handle non-finite values. No bound on the sum of `seq_valid` on one device may be relied on, other than what follows from the above.
Results may differ from a plain program's by a relative error of at most 0.00105.
The roundings to bfloat16 on the way count: a program that leaves them out, or rounds other values in their place, can miss the bound.
Values may be sent and summed in bfloat16 or wider, within the bound.
A program may use at most 128 MiB of HBM per device.

v0:
```python
import jax
import jax.numpy as jnp
from jax import lax
from jax.sharding import PartitionSpec as P

D = 512
H = 2
DK = 128
DV = 256
CONV = 4
SPAN = 64
STEP = 3


EPS_NORM = 1e-06
BETA_ONE = 0.9
BETA_TWO = 0.95
ADAM_EPS = 1e-08
LEARN_RATE = 0.01
WEIGHT_DECAY = 0.1
HIGHEST_ACCURACY = lax.Precision.HIGHEST


def split_small(small):
    channels = 2 * H * DK + H * DV
    first = D
    second = first + D * 2 * H
    third = second + CONV * channels
    fourth = third + H
    return (
        small[:first],
        small[first:second].reshape(D, 2 * H),
        small[second:third].reshape(CONV, channels),
        small[third:fourth],
        small[fourth:],
    )


def rms_gain(values, gain):
    return values * lax.rsqrt(jnp.mean(values * values, axis=-1, keepdims=True) + EPS_NORM) * gain


def features(projected, beta_gate, conv_taps, decay_log):
    channels = 2 * H * DK + H * DV
    length = projected.shape[0]
    padded = jnp.pad(projected[:, :channels], ((CONV - 1, 0), (0, 0)))
    convolved = conv_taps[0] * padded[0:length]
    for tap in range(1, CONV):
        convolved = convolved + conv_taps[tap] * padded[tap : tap + length]
    activated = jax.nn.silu(convolved)
    queries = activated[:, : H * DK].reshape(length, H, DK)
    key_rows = activated[:, H * DK : 2 * H * DK].reshape(length, H, DK)
    values = activated[:, 2 * H * DK :].reshape(length, H, DV)
    queries = (
        queries
        * lax.rsqrt(jnp.sum(queries * queries, axis=-1, keepdims=True) + EPS_NORM)
        * DK ** (-0.5)
    )
    key_rows = key_rows * lax.rsqrt(jnp.sum(key_rows * key_rows, axis=-1, keepdims=True) + EPS_NORM)
    betas = jax.nn.sigmoid(beta_gate[:, :H])
    log_decay = -jnp.exp(decay_log) * jax.nn.softplus(beta_gate[:, H:])
    return (queries, key_rows, values, betas, log_decay)


def finish(state_out, projected, out_gain):
    channels = 2 * H * DK + H * DV
    length = projected.shape[0]
    gate_part = projected[:, channels:].reshape(length, H, DV)
    return (rms_gain(state_out, out_gain) * jax.nn.silu(gate_part)).reshape(length, H * DV)


def tri_solve(matrix, right):
    return lax.linalg.triangular_solve(
        matrix, right, left_side=True, lower=True, unit_diagonal=True
    )


def blockwise(queries, key_rows, values, betas, log_decay):
    length = queries.shape[0]
    blocks = length // SPAN

    def regroup(array):
        return array.reshape((blocks, SPAN) + array.shape[1:]).swapaxes(1, 2)

    positions = jnp.arange(SPAN)
    lower_strict = positions[:, None] > positions[None, :]
    lower_incl = positions[:, None] >= positions[None, :]
    identity = jnp.eye(SPAN, dtype=jnp.float32)

    def one_block(memory_state, inputs):
        query_token_rows, key_block, value_rows, beta_rows, decay_rows = inputs
        cumulative = jnp.cumsum(decay_rows, axis=1)
        spread = cumulative[:, :, None] - cumulative[:, None, :]
        key_gram = jnp.einsum("hik,hjk->hij", key_block, key_block, precision=HIGHEST_ACCURACY)
        strict_decay = jnp.where(lower_strict, jnp.exp(jnp.where(lower_strict, spread, 0.0)), 0.0)
        incl_decay = jnp.where(lower_incl, jnp.exp(jnp.where(lower_incl, spread, 0.0)), 0.0)
        system = identity + beta_rows[:, :, None] * strict_decay * key_gram
        corrected_value = tri_solve(system, beta_rows[..., None] * value_rows)
        weighted_residual = tri_solve(
            system, (beta_rows * jnp.exp(cumulative))[..., None] * key_block
        )
        delta_residual = corrected_value - jnp.einsum(
            "yqo,yof->yqf", weighted_residual, memory_state, precision=HIGHEST_ACCURACY
        )
        scores = (
            jnp.einsum("hik,hjk->hij", query_token_rows, key_block, precision=HIGHEST_ACCURACY)
            * incl_decay
        )
        output = jnp.exp(cumulative)[..., None] * jnp.einsum(
            "yqo,yof->yqf", query_token_rows, memory_state, precision=HIGHEST_ACCURACY
        ) + jnp.einsum("hij,hjv->hiv", scores, delta_residual, precision=HIGHEST_ACCURACY)
        last_decay = cumulative[:, -1:]
        memory_state = jnp.exp(last_decay)[:, :, None] * memory_state + jnp.einsum(
            "ite,ito->ieo",
            key_block * jnp.exp(last_decay - cumulative)[..., None],
            delta_residual,
            precision=HIGHEST_ACCURACY,
        )
        return (memory_state, output)

    initial = jnp.zeros((H, DK, DV), jnp.float32)
    grouped = (
        regroup(queries),
        regroup(key_rows),
        regroup(values),
        regroup(betas),
        regroup(log_decay),
    )
    _, outputs = lax.scan(one_block, initial, grouped)
    return outputs.swapaxes(1, 2).reshape(length, H, DV)


def mixer(projected, beta_gate, conv_taps, decay_log, out_gain):

    def one_sequence(proj_rows, gate_rows):
        parts = features(proj_rows, gate_rows, conv_taps, decay_log)
        return finish(blockwise(*parts), proj_rows, out_gain)

    return jax.vmap(one_sequence)(projected, beta_gate)


def adamw(weight, grad, moment, second):
    moment_new = BETA_ONE * moment + (1.0 - BETA_ONE) * grad
    second_new = BETA_TWO * second + (1.0 - BETA_TWO) * grad * grad
    update = (
        moment_new
        / (1.0 - BETA_ONE**STEP)
        / (jnp.sqrt(second_new / (1.0 - BETA_TWO**STEP)) + ADAM_EPS)
    )
    return (weight - LEARN_RATE * (update + WEIGHT_DECAY * weight), moment_new, second_new)


def contract_last(left, right):
    return lax.dot_general(
        left, right, (((1,), (1,)), ((), ())), preferred_element_type=jnp.float32
    )


def contract_first(left, right):
    return lax.dot_general(
        left, right, (((0,), (0,)), ((), ())), preferred_element_type=jnp.float32
    )


def on_device(
    block_input,
    cotangent,
    seq_valid,
    in_weight,
    out_weight,
    small_params,
    in_moment,
    in_second,
    out_moment,
    out_second,
    small_moment,
    small_second,
):
    seq_here, length, width = block_input.shape
    total_rows = seq_here * length
    gain_in, beta_weight, conv_taps, decay_log, out_gain = split_small(small_params)
    in_bf = in_weight.astype(jnp.bfloat16)
    out_bf = out_weight.astype(jnp.bfloat16)
    proj_cols = in_weight.shape[1]
    mixed_cols = out_weight.shape[0] * lax.axis_size("fsdp")
    rows_f = block_input.reshape(total_rows, width).astype(jnp.float32)
    normed = rms_gain(rows_f, gain_in)
    normed_bf = normed.astype(jnp.bfloat16)
    columns = normed_bf
    projected = jnp.dot(
        columns,
        lax.all_gather(in_bf, "fsdp", axis=0, tiled=True),
        preferred_element_type=jnp.float32,
    )
    beta_gate = jnp.dot(normed, beta_weight, precision=HIGHEST_ACCURACY)
    mixed, mixer_back = jax.vjp(
        mixer,
        projected.reshape(seq_here, length, proj_cols),
        beta_gate.reshape(seq_here, length, 2 * H),
        conv_taps,
        decay_log,
        out_gain,
    )
    mixed_bf = mixed.reshape(total_rows, mixed_cols).astype(jnp.bfloat16)
    columns = mixed_bf
    branch_out = jnp.dot(
        columns,
        lax.all_gather(out_bf, "fsdp", axis=0, tiled=True),
        preferred_element_type=jnp.float32,
    )
    block_output = (rows_f + branch_out).reshape(seq_here, length, width)
    flags = seq_valid.astype(jnp.bfloat16)[:, None, None]
    upstream = (cotangent * flags).reshape(total_rows, width)
    d_mixed = contract_last(upstream, lax.all_gather(out_bf, "fsdp", axis=0, tiled=True))
    d_proj, d_beta, d_conv, d_decay, d_gain_out = mixer_back(
        d_mixed.reshape(seq_here, length, mixed_cols)
    )
    d_proj_bf = d_proj.reshape(total_rows, proj_cols).astype(jnp.bfloat16)
    d_beta = d_beta.reshape(total_rows, 2 * H)
    d_normed = contract_last(d_proj_bf, lax.all_gather(in_bf, "fsdp", axis=0, tiled=True))
    d_normed = d_normed + jnp.dot(d_beta, beta_weight.T, precision=HIGHEST_ACCURACY)
    _, norm_back = jax.vjp(rms_gain, rows_f, gain_in)
    d_rows, d_gain_in = norm_back(d_normed)
    input_grad = (upstream.astype(jnp.float32) + d_rows).reshape(seq_here, length, width)
    in_owned = lax.psum_scatter(
        contract_first(normed_bf, d_proj_bf), "fsdp", scatter_dimension=0, tiled=True
    )
    out_owned = lax.psum_scatter(
        contract_first(mixed_bf, upstream), "fsdp", scatter_dimension=0, tiled=True
    )
    in_grad, out_grad = lax.psum((in_owned, out_owned), "rep")
    small_local = jnp.concatenate(
        [
            d_gain_in,
            jnp.dot(normed.T, d_beta, precision=HIGHEST_ACCURACY).reshape(-1),
            d_conv.reshape(-1),
            d_decay,
            d_gain_out,
        ]
    )
    small_grad = lax.psum(small_local, ("rep", "fsdp"))
    new_in, in_m, in_v = adamw(in_weight, in_grad, in_moment, in_second)
    new_out, out_m, out_v = adamw(out_weight, out_grad, out_moment, out_second)
    new_small, small_m, small_v = adamw(small_params, small_grad, small_moment, small_second)
    return (
        block_output,
        input_grad,
        in_grad,
        out_grad,
        small_grad,
        new_in,
        new_out,
        new_small,
        in_m,
        in_v,
        out_m,
        out_v,
        small_m,
        small_v,
    )


def solution(mesh):
    in_specs = (
        P(("rep", "fsdp"), None, None),
        P(("rep", "fsdp"), None, None),
        P(("rep", "fsdp")),
        P("fsdp", None),
        P("fsdp", None),
        P(),
        P("fsdp", None),
        P("fsdp", None),
        P("fsdp", None),
        P("fsdp", None),
        P(),
        P(),
    )
    out_specs = (
        P(("rep", "fsdp"), None, None),
        P(("rep", "fsdp"), None, None),
        P("fsdp", None),
        P("fsdp", None),
        P(),
        P("fsdp", None),
        P("fsdp", None),
        P(),
        P("fsdp", None),
        P("fsdp", None),
        P("fsdp", None),
        P("fsdp", None),
        P(),
        P(),
    )
    return jax.shard_map(
        on_device, mesh=mesh, in_specs=in_specs, out_specs=out_specs, check_vma=False
    )
```

profile of v0, /device:TPU:0, one launch (start us, length us, event | category | flops | bytes accessed | tf_op | source)
XLA Modules:
  0.0 573.5 jit_solution(8990045714329149238)
XLA Ops:
  7.3 2.0 convert_element_type.62
  12.3 22.6 %all_gather.9 = bf16[512,512]{1,0:T(8,128)(2,1)S(1)} all-gather(bf16[128,512]{1,0:T(8,128)(2,1)S(1)} %convert_element_type.65), channel_id=1, replica_groups=mesh['rep'=8,'fsdp'=4] {'fsdp'}, dimensions={0}, use_global_device_ids=true | all-gather | bytes 655360 | tf_op jit(solution)/shard_map/all_gather | solution.py:208
  37.1 16.6 %all-gather.2.cloned.1.call-done = bf16[512,1536]{1,0:T(8,128)(2,1)} async-done(((bf16[128,1536]{1,0:T(8,128)(2,1)}), bf16[512,1536]{1,0:T(8,128)(2,1)}) %all-gather.2.cloned.1.call-update) | async-done | bytes 1572880 | tf_op jit(solution)/shard_map/all_gather | solution.py:192
  53.8 2.0 convolution_bitcast_fusion.10
  57.1 1.6 fusion.204
  67.1 1.9 copy.335
  72.9 89.8 %while.93 = (s32[]{:T(128)}, f32[1,2,128,256]{3,2,1,0:T(8,128)S(1)}, f32[4,1,2,64,256]{4,3,2,1,0:T(8,128)S(1)}, f32[4,1,2,64,64]{4,3,2,1,0:T(8,128)}, f32[4,1,2,...) while((s32[]{:T(128)}, ...), condition=%wide.region_5.6_spmd.clone.clone, body=%wide.region_3.5_spmd.clone.clone.sunk | while | flops 239899200 | bytes 5005722 | solution.py:129
  75.4 9.8 %custom-call.55 = f32[1,2,1,64,64]{3,4,2,1,0:T(8,128)S(1)} custom-call(f32[1,2,1,64,64]{4,3,2,1,0:T(8,128)S(1)} %add_bitcast_fusion.5), custom_call_target="InvertDiagBlocksLowerTriangular" | custom-call | tf_op jit(solution)/shard_map/jvp(vmap())/while/body/eval_jaxpr/triangular_solve | solution.py:73
  85.2 1.9 bitcast_dynamic-update-slice_fusion.17
  97.8 9.8 %custom-call.55 = f32[1,2,1,64,64]{3,4,2,1,0:T(8,128)S(1)} custom-call(f32[1,2,1,64,64]{4,3,2,1,0:T(8,128)S(1)} %add_bitcast_fusion.5), custom_call_target="InvertDiagBlocksLowerTriangular" | custom-call | tf_op jit(solution)/shard_map/jvp(vmap())/while/body/eval_jaxpr/triangular_solve | solution.py:73
  107.7 1.9 bitcast_dynamic-update-slice_fusion.17
  120.3 9.8 %custom-call.55 = f32[1,2,1,64,64]{3,4,2,1,0:T(8,128)S(1)} custom-call(f32[1,2,1,64,64]{4,3,2,1,0:T(8,128)S(1)} %add_bitcast_fusion.5), custom_call_target="InvertDiagBlocksLowerTriangular" | custom-call | tf_op jit(solution)/shard_map/jvp(vmap())/while/body/eval_jaxpr/triangular_solve | solution.py:73
  130.1 1.9 bitcast_dynamic-update-slice_fusion.17
  137.1 1.3 constant_dynamic-update-slice_fusion.15
  142.8 9.8 %custom-call.55 = f32[1,2,1,64,64]{3,4,2,1,0:T(8,128)S(1)} custom-call(f32[1,2,1,64,64]{4,3,2,1,0:T(8,128)S(1)} %add_bitcast_fusion.5), custom_call_target="InvertDiagBlocksLowerTriangular" | custom-call | tf_op jit(solution)/shard_map/jvp(vmap())/while/body/eval_jaxpr/triangular_solve | solution.py:73
  152.6 1.9 bitcast_dynamic-update-slice_fusion.17
  159.6 1.3 constant_dynamic-update-slice_fusion.15
  164.6 2.3 fusion.224
  166.9 1.4 reshape.2011
  168.2 2.6 multiply_reduce_fusion.5
  174.6 232.8 %while.94 = (s32[]{:T(128)}, f32[1,2,128,256]{2,3,1,0:T(8,128)S(1)}, f32[4,1,2,64,128]{4,3,0,2,1:T(8,128)}, f32[4,1,2,64,128]{4,3,0,2,1:T(8,128)}, f32[4,1,2,64,...) while((s32[]{:T(128)}, ...), condition=%wide.region_19.21_spmd.clone.clone, body=%wide.region_8.20_spmd.clone.clone.sunk | while | flops 492074048 | bytes 10320584 | solution.py:129
  181.5 9.8 %custom-call.56 = f32[1,2,1,64,64]{3,4,2,1,0:T(8,128)S(1)} custom-call(f32[1,2,1,64,64]{4,3,2,1,0:T(8,128)S(1)} %fusion.403), custom_call_target="InvertDiagBlocksLowerTriangular" | custom-call | tf_op jit(solution)/shard_map/transpose(jvp(vmap()))/while/body/eval_jaxpr/triangular_solve/custom-call.3 | solution.py:73
  193.9 1.9 fusion.408
  197.2 9.8 %custom-call.57 = f32[1,2,1,64,64]{3,4,2,1,0:T(8,128)S(1)} custom-call(f32[1,2,1,64,64]{4,3,2,1,0:T(8,128)S(1)} %add_bitcast_fusion.6), custom_call_target="InvertDiagBlocksLowerTriangular" | custom-call | tf_op jit(solution)/shard_map/transpose(jvp(vmap()))/while/body/eval_jaxpr/triangular_solve | solution.py:73
  211.6 1.4 copy.345
  217.2 1.4 fusion.418
  218.6 1.6 reduce_window_sum.50
  220.2 1.7 bitcast_dynamic-update-slice_fusion.23
  230.0 1.4 convolution_bitcast_fusion.17
  239.8 9.8 %custom-call.56 = f32[1,2,1,64,64]{3,4,2,1,0:T(8,128)S(1)} custom-call(f32[1,2,1,64,64]{4,3,2,1,0:T(8,128)S(1)} %fusion.403), custom_call_target="InvertDiagBlocksLowerTriangular" | custom-call | tf_op jit(solution)/shard_map/transpose(jvp(vmap()))/while/body/eval_jaxpr/triangular_solve/custom-call.3 | solution.py:73
  252.1 1.9 fusion.408
  255.4 9.8 %custom-call.57 = f32[1,2,1,64,64]{3,4,2,1,0:T(8,128)S(1)} custom-call(f32[1,2,1,64,64]{4,3,2,1,0:T(8,128)S(1)} %add_bitcast_fusion.6), custom_call_target="InvertDiagBlocksLowerTriangular" | custom-call | tf_op jit(solution)/shard_map/transpose(jvp(vmap()))/while/body/eval_jaxpr/triangular_solve | solution.py:73
  269.7 1.4 copy.345
  275.3 1.4 fusion.418
  276.7 1.6 reduce_window_sum.50
  278.4 1.7 bitcast_dynamic-update-slice_fusion.23
  288.1 1.4 convolution_bitcast_fusion.17
  297.9 9.8 %custom-call.56 = f32[1,2,1,64,64]{3,4,2,1,0:T(8,128)S(1)} custom-call(f32[1,2,1,64,64]{4,3,2,1,0:T(8,128)S(1)} %fusion.403), custom_call_target="InvertDiagBlocksLowerTriangular" | custom-call | tf_op jit(solution)/shard_map/transpose(jvp(vmap()))/while/body/eval_jaxpr/triangular_solve/custom-call.3 | solution.py:73
  310.2 1.9 fusion.408
  313.6 9.8 %custom-call.57 = f32[1,2,1,64,64]{3,4,2,1,0:T(8,128)S(1)} custom-call(f32[1,2,1,64,64]{4,3,2,1,0:T(8,128)S(1)} %add_bitcast_fusion.6), custom_call_target="InvertDiagBlocksLowerTriangular" | custom-call | tf_op jit(solution)/shard_map/transpose(jvp(vmap()))/while/body/eval_jaxpr/triangular_solve | solution.py:73
  327.9 1.4 copy.345
  333.5 1.4 fusion.418
  334.9 1.6 reduce_window_sum.50
  336.6 1.7 bitcast_dynamic-update-slice_fusion.23
  339.3 1.3 constant_dynamic-update-slice_fusion.19
  346.4 1.4 convolution_bitcast_fusion.17
  356.1 9.8 %custom-call.56 = f32[1,2,1,64,64]{3,4,2,1,0:T(8,128)S(1)} custom-call(f32[1,2,1,64,64]{4,3,2,1,0:T(8,128)S(1)} %fusion.403), custom_call_target="InvertDiagBlocksLowerTriangular" | custom-call | tf_op jit(solution)/shard_map/transpose(jvp(vmap()))/while/body/eval_jaxpr/triangular_solve/custom-call.3 | solution.py:73
  368.5 1.9 fusion.408
  371.8 9.8 %custom-call.57 = f32[1,2,1,64,64]{3,4,2,1,0:T(8,128)S(1)} custom-call(f32[1,2,1,64,64]{4,3,2,1,0:T(8,128)S(1)} %add_bitcast_fusion.6), custom_call_target="InvertDiagBlocksLowerTriangular" | custom-call | tf_op jit(solution)/shard_map/transpose(jvp(vmap()))/while/body/eval_jaxpr/triangular_solve | solution.py:73
  386.2 1.4 copy.345
  391.8 1.4 fusion.418
  393.2 1.6 reduce_window_sum.50
  394.8 1.7 bitcast_dynamic-update-slice_fusion.23
  397.6 1.3 constant_dynamic-update-slice_fusion.19
  404.6 1.4 convolution_bitcast_fusion.17
  420.3 1.7 add_add_fusion.3
  422.6 1.9 multiply_reduce_fusion.3
  426.1 2.3 fusion.236
  430.7 2.2 fusion.262
  433.9 44.8 %psum.23 = f32[6914]{0:T(1024)S(1)} all-reduce(f32[6914]{0:T(1024)S(1)} %concatenate.3), channel_id=1, replica_groups=mesh['rep'=8,'fsdp'=4] {'rep','fsdp'}, use_global_device_ids=true, to_apply=%region_34.36 | all-reduce | flops 6914 | bytes 55312 | tf_op jit(solution)/shard_map/psum | solution.py:241
  479.4 21.4 %reduce-scatter.3.cloned.1.call-done = f32[128,1536]{1,0:T(8,128)} async-done(((f32[512,1536]{1,0:T(8,128)}), f32[128,1536]{1,0:T(8,128)}) %reduce-scatter.3.cloned.1.call-update) | async-done | bytes 786448 | tf_op jit(solution)/shard_map/reduce_scatter | solution.py:225
  501.8 2.6 fusion.201
  504.4 56.1 %all-reduce.20.cloned.1.call-done = (f32[128,1536]{1,0:T(8,128)}, f32[128,512]{1,0:T(8,128)}) async-done(((f32[128,1536]{1,0:T(8,128)}, f32[128,512]{1,0:T(8,128)}), (f32[128,1536]{1,0:T(8,128)}, f32[128,512]{1,0:T(8,128)})) %all-reduce.20.cloned.1.call-update) | async-done | bytes 1048592 | tf_op jit(solution)/shard_map/psum | solution.py:231
  560.5 3.5 multiply_subtract_fusion
  (518 shorter events, 198.8 us)
Async XLA Ops:
  7.2 2.1 copy-start.33
  7.2 2.7 copy-start
  7.2 5.0 copy-start.22
  7.2 46.5 %all-gather.2.cloned.1.call-start = ((), (), s32[]{:S(2)}) async-start(), calls=%async_computation.2 | async-start | bytes 1966080 | tf_op jit(solution)/shard_map/all_gather | solution.py:192
  9.2 25.7 %copy-start.12 = (bf16[1,256,512]{2,1,0:T(8,128)(2,1)S(1)}, bf16[1,256,512]{2,1,0:T(8,128)(2,1)}, u32[]{:S(2)}) copy-start(bf16[1,256,512]{2,1,0:T(8,128)(2,1)} %param.19) | copy-start | bytes 786436
  9.3 470.2 %reduce-scatter.5.cloned.1.call-start = ((), (), s32[]{:S(2)}) async-start(), calls=%async_computation.4 | async-start | bytes 1310720 | tf_op jit(solution)/shard_map/reduce_scatter | solution.py:228
  9.3 44.4 %copy-start.35 = (f32[512]{0:T(512)}, f32[512]{0:T(512)S(1)}, u32[]{:S(2)}) copy-start(f32[512]{0:T(512)S(1)} %slice.100) | copy-start | bytes 6148
  9.9 25.0 %copy-start.14 = (f32[512,4]{1,0:T(8,128)}, f32[512,4]{1,0:T(8,128)S(1)}, u32[]{:S(2)}) copy-start(f32[512,4]{1,0:T(8,128)S(1)} %reshape.1997) | copy-start | bytes 24580
  10.0 43.7 %copy-start.37 = (f32[256]{0:T(256)}, f32[256]{0:T(256)S(1)}, u32[]{:S(2)}) copy-start(f32[256]{0:T(256)S(1)} %fusion.275) | copy-start | bytes 3076
  10.7 1.6 copy-start.49
  10.7 25.7 %copy-start.64 = (f32[2]{0:T(128)}, f32[2]{0:T(128)S(1)}, u32[]{:S(2)}) copy-start(f32[2]{0:T(128)S(1)} %fusion.276) | copy-start | bytes 28
  10.8 1.5 copy-start.55
  12.3 151.6 %copy-start.61 = (f32[1,2,2,128]{3,1,2,0:T(2,128)}, f32[1,2,2,128]{3,1,2,0:T(2,128)S(1)}, u32[]{:S(2)}) copy-start(f32[1,2,2,128]{3,1,2,0:T(2,128)S(1)} %copy.310) | copy-start | bytes 6148
  34.9 20.9 %copy-start.17 = (bf16[512,512]{1,0:T(8,128)(2,1)}, bf16[512,512]{1,0:T(8,128)(2,1)S(1)}, u32[]{:S(2)}) copy-start(bf16[512,512]{1,0:T(8,128)(2,1)S(1)} %all_gather.9) | copy-start | bytes 1572868
  35.2 20.6 %copy-start.6 = (f32[256,512]{1,0:T(8,128)}, f32[256,512]{1,0:T(8,128)S(1)}, u32[]{:S(2)}) copy-start(f32[256,512]{1,0:T(8,128)S(1)} %fusion.243) | copy-start | bytes 1572868
  37.1 20.0 %copy-start.39 = (f32[1024]{0:T(1024)}, f32[1024]{0:T(1024)S(1)}, u32[]{:S(2)}) copy-start(f32[1024]{0:T(1024)S(1)} %get-tuple-element.2429) | copy-start | bytes 12292
  37.1 20.0 %copy-start.41 = (f32[1024]{0:T(1024)}, f32[1024]{0:T(1024)S(1)}, u32[]{:S(2)}) copy-start(f32[1024]{0:T(1024)S(1)} %get-tuple-element.2430) | copy-start | bytes 12292
  37.1 20.0 %copy-start.43 = (f32[1024]{0:T(1024)}, f32[1024]{0:T(1024)S(1)}, u32[]{:S(2)}) copy-start(f32[1024]{0:T(1024)S(1)} %get-tuple-element.2431) | copy-start | bytes 12292
  37.1 20.0 %copy-start.45 = (f32[1024]{0:T(1024)}, f32[1024]{0:T(1024)S(1)}, u32[]{:S(2)}) copy-start(f32[1024]{0:T(1024)S(1)} %get-tuple-element.2432) | copy-start | bytes 12292
  64.4 4.6 copy-start.51
  65.7 3.3 copy-start.53
  163.4 3.4 copy-start.19
  163.9 3.0 copy-start.20
  193.8 13.2 %copy-start.30 = (f32[2,64]{1,0:T(2,128)}, f32[2,64]{1,0:T(2,128)S(1)}, u32[]{:S(2)}) copy-start(f32[2,64]{1,0:T(2,128)S(1)} %fusion.400) | copy-start | bytes 1540 | tf_op jit(solution)/shard_map/transpose(jvp(vmap()))/while
  207.1 3.0 copy-start.4
  211.6 16.3 %copy-start.21 = (f32[4,1,2,64,64]{4,3,2,1,0:T(8,128)S(1)}, f32[4,1,2,64,64]{4,3,2,1,0:T(8,128)}, u32[]{:S(2)}) copy-start(f32[4,1,2,64,64]{4,3,2,1,0:T(8,128)} %get-tuple-element.3172) | copy-start | bytes 393220 | tf_op jit(solution)/shard_map/transpose(jvp(vmap()))/while
  252.1 13.2 %copy-start.30 = (f32[2,64]{1,0:T(2,128)}, f32[2,64]{1,0:T(2,128)S(1)}, u32[]{:S(2)}) copy-start(f32[2,64]{1,0:T(2,128)S(1)} %fusion.400) | copy-start | bytes 1540 | tf_op jit(solution)/shard_map/transpose(jvp(vmap()))/while
  265.3 2.9 copy-start.4
  269.7 16.2 %copy-start.21 = (f32[4,1,2,64,64]{4,3,2,1,0:T(8,128)S(1)}, f32[4,1,2,64,64]{4,3,2,1,0:T(8,128)}, u32[]{:S(2)}) copy-start(f32[4,1,2,64,64]{4,3,2,1,0:T(8,128)} %get-tuple-element.3172) | copy-start | bytes 393220 | tf_op jit(solution)/shard_map/transpose(jvp(vmap()))/while
  310.2 13.2 %copy-start.30 = (f32[2,64]{1,0:T(2,128)}, f32[2,64]{1,0:T(2,128)S(1)}, u32[]{:S(2)}) copy-start(f32[2,64]{1,0:T(2,128)S(1)} %fusion.400) | copy-start | bytes 1540 | tf_op jit(solution)/shard_map/transpose(jvp(vmap()))/while
  323.4 3.0 copy-start.4
  327.9 16.3 %copy-start.21 = (f32[4,1,2,64,64]{4,3,2,1,0:T(8,128)S(1)}, f32[4,1,2,64,64]{4,3,2,1,0:T(8,128)}, u32[]{:S(2)}) copy-start(f32[4,1,2,64,64]{4,3,2,1,0:T(8,128)} %get-tuple-element.3172) | copy-start | bytes 393220 | tf_op jit(solution)/shard_map/transpose(jvp(vmap()))/while
  368.5 13.2 %copy-start.30 = (f32[2,64]{1,0:T(2,128)}, f32[2,64]{1,0:T(2,128)S(1)}, u32[]{:S(2)}) copy-start(f32[2,64]{1,0:T(2,128)S(1)} %fusion.400) | copy-start | bytes 1540 | tf_op jit(solution)/shard_map/transpose(jvp(vmap()))/while
  381.7 3.0 copy-start.4
  386.2 16.2 %copy-start.21 = (f32[4,1,2,64,64]{4,3,2,1,0:T(8,128)S(1)}, f32[4,1,2,64,64]{4,3,2,1,0:T(8,128)}, u32[]{:S(2)}) copy-start(f32[4,1,2,64,64]{4,3,2,1,0:T(8,128)} %get-tuple-element.3172) | copy-start | bytes 393220 | tf_op jit(solution)/shard_map/transpose(jvp(vmap()))/while
  407.4 2.3 copy-start.13
  409.7 1.7 copy-start.16
  409.7 1.7 copy-start.25
  409.7 1.7 copy-start.26
  409.7 1.9 copy-start.54
  411.1 89.7 %reduce-scatter.3.cloned.1.call-start = ((), (), s32[]{:S(2)}) async-start(), calls=%async_computation.3 | async-start | bytes 3932160 | tf_op jit(solution)/shard_map/reduce_scatter | solution.py:225
  411.4 2.4 copy-start.52
  412.3 4.0 copy-start.11
  413.8 3.7 copy-start.27
  415.2 3.5 copy-start.18
  420.3 2.0 copy-start.2
  420.3 2.2 copy-start.8
  422.5 1.9 copy-start.40
  422.5 1.9 copy-start.42
  422.6 1.9 copy-start.44
  422.6 1.9 copy-start.46
  428.4 2.2 copy-start.34
  428.5 132.0 %all-reduce.20.cloned.1.call-start = ((), (), s32[]{:S(2)}) async-start(), calls=%async_computation.5 | async-start | bytes 2097152 | tf_op jit(solution)/shard_map/psum | solution.py:231
  430.7 2.2 copy-start.15
  433.0 45.8 %copy-start.60 = (f32[256]{0:T(256)S(1)}, f32[256]{0:T(256)}, u32[]{:S(2)}) copy-start(f32[256]{0:T(256)} %copy-done.59) | copy-start | bytes 3076
  433.0 45.8 %copy-start.47 = (f32[6914]{0:T(1024)S(1)}, f32[6914]{0:T(1024)}, u32[]{:S(2)}) copy-start(f32[6914]{0:T(1024)} %param.28) | copy-start | bytes 82972
  433.0 45.8 %copy-start.48 = (f32[6914]{0:T(1024)S(1)}, f32[6914]{0:T(1024)}, u32[]{:S(2)}) copy-start(f32[6914]{0:T(1024)} %param.29) | copy-start | bytes 82972
  433.9 68.0 %copy-start.62 = (f32[1,2,2,128]{3,1,2,0:T(2,128)S(1)}, f32[1,2,2,128]{3,1,2,0:T(2,128)}, u32[]{:S(2)}) copy-start(f32[1,2,2,128]{3,1,2,0:T(2,128)} %copy-done.61) | copy-start | bytes 6148
  478.7 25.7 %copy-start.32 = (f32[6914]{0:T(1024)}, f32[6914]{0:T(1024)S(1)}, u32[]{:S(2)}) copy-start(f32[6914]{0:T(1024)S(1)} %psum.23) | copy-start | bytes 82972
  501.8 58.7 %copy-start.9 = (f32[128,1536]{1,0:T(8,128)S(1)}, f32[128,1536]{1,0:T(8,128)}, u32[]{:S(2)}) copy-start(f32[128,1536]{1,0:T(8,128)} %param.21) | copy-start | bytes 2359300
  560.5 3.5 copy-start.23
  560.5 3.5 copy-start.24
  560.5 3.5 copy-start.28
  560.5 3.5 copy-start.29
  (18 other events, 17.5 us)
Sparse Core Ops, SparseCore 0:
  10.2 43.5 all-gather.1
  411.2 27.2 reduce-scatter.4
  440.8 59.9 reduce-scatter.2
  503.9 56.5 all-reduce.19
where the time goes:
time: 578 us; the launch traced here: 574 us
  other arithmetic  204 us (35%)
  matrix products  116 us (20%)
  waiting for transfers between devices  94.2 us (16%)
  local copies, waits for them, and re-layouts  75.1 us (13%)
  blocking collectives  67.3 us (12%)
  between operations  15.6 us (3%)
    another operation x44, other arithmetic, tri_solve(): lax.linalg.triangular_solve(matrix, right, left_side=True, lower=True, un...  126 us
    psum x1, waiting for transfers between devices, on_device(): in_grad, out_grad = lax.psum((in_owned, out_owned), 'rep')  56.1 us
    psum x1, blocking collectives, on_device(): small_grad = lax.psum(small_local, ('rep', 'fsdp'))  44.8 us
    another operation x24, matrix products, tri_solve(): lax.linalg.triangular_solve(matrix, right, left_side=True, lower=True, un...  29.1 us
    all_gather x1, blocking collectives, on_device(): lax.all_gather(out_bf, 'fsdp', axis=0, tiled=True)  22.6 us
    reduce_scatter x1, waiting for transfers between devices, on_device(): lax.psum_scatter(contract_first(normed_bf, d_proj_bf), 'fsdp', scatter_di...  21.4 us
    dynamic_update_slice x20, other arithmetic, blockwise(): _, outputs = lax.scan(one_block, initial, grouped)  18.6 us
    all_gather x1, waiting for transfers between devices, on_device(): lax.all_gather(in_bf, 'fsdp', axis=0, tiled=True)  16.6 us
  transfers between devices with their start and end apart: 4, of which 3 were waited for; matrix products, arithmetic and copies ran while one was open for 5% of the time, Pallas kernels for 0%

commit v1 on v0

v1 whole, which is shorter than its diff:
```python
import functools

import jax
import jax.numpy as jnp
from jax import lax
from jax.experimental import pallas as pl
from jax.experimental.pallas import tpu as pltpu
from jax.sharding import PartitionSpec as P

D = 512
H = 2
DK = 128
DV = 256
CONV = 4
CHUNK = 128
STEP = 3


EPS_NORM = 1e-06
BETA_ONE = 0.9
BETA_TWO = 0.95
ADAM_EPS = 1e-08
LEARN_RATE = 0.01
WEIGHT_DECAY = 0.1


def split_small(small):
    channels = 2 * H * DK + H * DV
    first = D
    second = first + D * 2 * H
    third = second + CONV * channels
    fourth = third + H
    return (
        small[:first],
        small[first:second].reshape(D, 2 * H),
        small[second:third].reshape(CONV, channels),
        small[third:fourth],
        small[fourth:],
    )


def split(value):
    high = value.astype(jnp.bfloat16)
    return (high, (value - high.astype(jnp.float32)).astype(jnp.bfloat16))


def dot(left, right, left_dim=1, right_dim=0):
    return lax.dot_general(
        left,
        right,
        (((left_dim,), (right_dim,)), ((), ())),
        preferred_element_type=jnp.float32,
    )


def dot3(left, right, left_dim=1, right_dim=0):
    return (
        dot(left[0], right[1], left_dim, right_dim)
        + dot(left[1], right[0], left_dim, right_dim)
    ) + dot(left[0], right[0], left_dim, right_dim)


def row_sum(value):
    return jnp.sum(value, axis=1, keepdims=True)


def col_sum(value):
    return jnp.sum(value, axis=0, keepdims=True)


def sigmoid(value):
    return 1.0 / (1.0 + jnp.exp(-value))


def total(*terms):
    out = None
    for term in terms:
        if term is not None:
            out = term if out is None else out + term
    return out


def unit_inverse(strict, levels, level_masks):
    size = strict[0].shape[0]
    rows = lax.broadcasted_iota(jnp.int32, (size, size), 0)
    cols = lax.broadcasted_iota(jnp.int32, (size, size), 1)
    eye = jnp.where(rows == cols, 1.0, 0.0)
    inverses = [eye - jnp.where(level_masks[0], a, 0.0) for a in strict]
    for level in range(1, levels):
        for n, a in enumerate(strict):
            inv = split(inverses[n])
            inner = dot3(inv, split(jnp.where(level_masks[level], a, 0.0)))
            inverses[n] = inverses[n] - dot3(split(inner), inv)
    return inverses


def local_kernel(
    flag_ref,
    x_ref,
    cot_ref,
    win_ref,
    wout_ref,
    gain_ref,
    bw_ref,
    taps_ref,
    dlog_ref,
    ogain_ref,
    out_ref,
    xgrad_ref,
    gin_ref,
    gout_ref,
    dgain_ref,
    dbw_ref,
    dtaps_ref,
    ddlog_ref,
    dogain_ref,
    proj_ref,
    conv_ref,
    mixed_ref,
    dproj_ref,
    dact_ref,
    *,
    seqs,
):
    f32, bf16 = jnp.float32, jnp.bfloat16
    length, width = x_ref.shape[1:]
    channels = taps_ref.shape[1]
    lanes = bw_ref.shape[1]
    chunk = CHUNK if length % CHUNK == 0 else length
    chunks = length // chunk

    def keep(ref, value):
        if seqs == 1:
            ref[...] = value
        else:

            @pl.when(pl.program_id(0) == 0)
            def _():
                ref[...] = value

            @pl.when(pl.program_id(0) > 0)
            def _():
                ref[...] = ref[...] + value

    gain = gain_ref[...]
    x = x_ref[0].astype(f32)
    x_scale = lax.rsqrt(jnp.mean(x * x, axis=1, keepdims=True) + EPS_NORM)
    x_hat = x * x_scale
    normed = x_hat * gain
    normed_bf = normed.astype(bf16)
    normed_s = (normed_bf, (normed - normed_bf.astype(f32)).astype(bf16))
    proj_ref[...] = dot(normed_bf, win_ref[...])
    bw_s = split(bw_ref[...])
    gate = dot3(normed_s, bw_s)
    gate_sig = sigmoid(gate)
    decay_rate = -jnp.exp(dlog_ref[...])
    softplus = jnp.maximum(gate, 0.0) + jnp.log1p(jnp.exp(-jnp.abs(gate)))
    log_decay = decay_rate * softplus

    row_id = lax.broadcasted_iota(jnp.int32, (length, DK), 0)

    def shifted(value, by):
        if by == 0:
            return value
        rolled = pltpu.roll(value, by % length, axis=0)
        if by > 0:
            return jnp.where(row_id >= by, rolled, 0.0)
        return jnp.where(row_id < length + by, rolled, 0.0)

    def conv_block(at):
        piece = proj_ref[:, at : at + DK]
        acc = None
        for tap in range(CONV):
            term = taps_ref[tap : tap + 1, at : at + DK] * shifted(piece, CONV - 1 - tap)
            acc = term if acc is None else acc + term
        return acc

    for at in range(0, channels, DK):
        conv_ref[:, at : at + DK] = conv_block(at)

    def active(at, wide):
        value = conv_ref[:, at : at + wide]
        return value * sigmoid(value)

    rows = lax.broadcasted_iota(jnp.int32, (chunk, chunk), 0)
    cols = lax.broadcasted_iota(jnp.int32, (chunk, chunk), 1)
    lower_strict = rows > cols
    lower_incl = rows >= cols
    ones_lower = jnp.where(lower_incl, 1.0, 0.0).astype(bf16)
    levels = chunk.bit_length() - 1
    level_masks = [
        ((rows >> level) ^ (cols >> level)) == 1 for level in range(levels)
    ]

    def exact_sum(value, dim):
        high = value.astype(bf16)
        rest = value - high.astype(f32)
        mid = rest.astype(bf16)
        low = (rest - mid.astype(f32)).astype(bf16)
        return (
            dot(ones_lower, low, dim, 0) + dot(ones_lower, mid, dim, 0)
        ) + dot(ones_lower, high, dim, 0)

    cums = [exact_sum(log_decay[c * chunk : (c + 1) * chunk], 1) for c in range(chunks)]
    cums_t = [jnp.transpose(cum) for cum in cums]

    scale = DK ** (-0.5)
    q_hat, q_rs, k_hat, k_rs, vals = ([], [], [], [], [])
    for h in range(H):
        q = active(h * DK, DK)
        k = active((H + h) * DK, DK)
        q_rs.append(lax.rsqrt(row_sum(q * q) + EPS_NORM))
        k_rs.append(lax.rsqrt(row_sum(k * k) + EPS_NORM))
        q_hat.append(q * q_rs[h])
        k_hat.append(k * k_rs[h])
        vals.append(active(2 * H * DK + h * DV, DV))

    units = [(h, c) for h in range(H) for c in range(chunks)]
    info = {}
    for h, c in units:
        span = slice(c * chunk, (c + 1) * chunk)
        k = k_hat[h][span]
        q = q_hat[h][span] * scale
        u = {"k": k, "q": q, "ks": split(k), "qs": split(q), "v": vals[h][span]}
        u["beta"] = gate_sig[span, h : h + 1]
        g = cums[c][:, H + h : H + h + 1]
        g_row = cums_t[c][H + h : H + h + 1, :]
        spread = g - g_row
        u["incl"] = jnp.where(lower_incl, jnp.exp(jnp.where(lower_incl, spread, 0.0)), 0.0)
        u["strict"] = jnp.where(lower_strict, u["incl"], 0.0)
        u["eg"] = jnp.exp(g)
        last = g[chunk - 1 : chunk]
        u["elast"] = jnp.exp(last)
        u["tail"] = jnp.exp(last - g)
        u["a"] = u["beta"] * u["strict"] * dot3(u["ks"], u["ks"], 1, 1)
        u["p"] = split(u["incl"] * dot3(u["qs"], u["ks"], 1, 1))
        info[h, c] = u
    inverses = unit_inverse([info[n]["a"] for n in units], levels, level_masks)
    for n, inverse in zip(units, inverses):
        info[n]["t"] = split(inverse)

    state_out = {}
    for h in range(H):
        state = None
        for c in range(chunks):
            u = info[h, c]
            u["s"] = state
            u["ss"] = None if state is None else split(state)
            if state is None:
                u["e"] = u["v"]
            else:
                u["e"] = u["v"] - u["eg"] * dot3(u["ks"], u["ss"])
            delta = dot3(u["t"], split(u["beta"] * u["e"]))
            u["d"] = split(delta)
            o = dot3(u["p"], u["d"])
            if state is not None:
                o = o + u["eg"] * dot3(u["qs"], u["ss"])
            state_out[h, c] = o
            if c < chunks - 1:
                u["kd"] = split(u["k"] * u["tail"])
                update = dot3(u["kd"], u["d"], 0, 0)
                state = update if state is None else u["elast"] * state + update

    flag = flag_ref[pl.program_id(0)].astype(f32)
    upstream_f = cot_ref[0].astype(f32) * flag
    upstream = upstream_f.astype(bf16)
    ogain = ogain_ref[...]
    o_grads = {}
    d_ogain = None
    for h in range(H):
        o = jnp.concatenate([state_out[h, c] for c in range(chunks)], axis=0)
        o_rs = lax.rsqrt(jnp.mean(o * o, axis=1, keepdims=True) + EPS_NORM)
        o_hat = o * o_rs
        at = channels + h * DV
        z = proj_ref[:, at : at + DV]
        z_sig = sigmoid(z)
        z_act = z * z_sig
        gained = o_hat * ogain
        mixed_ref[:, h * DV : (h + 1) * DV] = (gained * z_act).astype(bf16)
        d_mixed = dot(upstream, wout_ref[h * DV : (h + 1) * DV, :], 1, 1)
        d_z = d_mixed * gained * (z_sig * (1.0 + z * (1.0 - z_sig)))
        dproj_ref[:, at : at + DV] = d_z.astype(bf16)
        d_gained = d_mixed * z_act
        d_ogain = total(d_ogain, col_sum(d_gained * o_hat))
        d_hat = d_gained * ogain
        d_o = o_rs * (d_hat - o_hat * jnp.mean(o_hat * d_hat, axis=1, keepdims=True))
        for c in range(chunks):
            o_grads[h, c] = d_o[c * chunk : (c + 1) * chunk]
    keep(dogain_ref, d_ogain)
    out_ref[0] = x + dot(mixed_ref[...], wout_ref[...])
    keep(gout_ref, dot(mixed_ref[...], upstream, 0, 0))

    d_beta_cols = {}
    d_cum_cols = {}
    for h in range(H):
        d_state = None
        d_q_parts, d_k_parts = ([None] * chunks, [None] * chunks)
        for c in reversed(range(chunks)):
            u = info[h, c]
            span = slice(c * chunk, (c + 1) * chunk)
            d_o = o_grads[h, c]
            d_os = split(d_o)
            d_d = dot3(u["p"], d_os, 0, 0)
            d_qk = split(u["incl"] * dot3(d_os, u["d"], 1, 1))
            d_q = dot3(d_qk, u["ks"])
            d_k_minus = dot3(d_qk, u["qs"], 0, 0)
            d_k_plus = None
            d_last = None
            new_d_state = None
            if d_state is not None:
                d_ss = split(d_state)
                d_kd = u["tail"] * dot3(u["d"], d_ss, 1, 1)
                d_d = d_d + dot3(u["kd"], d_ss)
                d_k_minus = d_k_minus + d_kd
                d_last = jnp.sum(row_sum(u["k"] * d_kd), axis=0, keepdims=True)
                if u["s"] is not None:
                    d_last = d_last + u["elast"] * jnp.sum(
                        row_sum(u["s"] * d_state), axis=0, keepdims=True
                    )
                    new_d_state = u["elast"] * d_state
            d_r = dot3(u["t"], split(d_d), 0, 0)
            d_rs = split(d_r)
            hold = split(-u["strict"] * dot3(d_rs, u["d"], 1, 1))
            hold_k = dot3(hold, u["ks"])
            d_beta = row_sum(d_r * u["e"]) + row_sum(u["k"] * hold_k)
            d_k_plus = u["beta"] * hold_k
            d_k_minus = d_k_minus + dot3(hold, split(u["beta"] * u["k"]), 0, 0)
            d_e = u["beta"] * d_r
            dact_ref[span, 2 * H * DK + h * DV : 2 * H * DK + (h + 1) * DV] = d_e
            if u["s"] is not None:
                d_os_g = split(u["eg"] * d_o)
                d_es_g = split(-u["eg"] * d_e)
                d_q = d_q + dot3(d_os_g, u["ss"], 1, 1)
                d_k_plus = d_k_plus + dot3(d_es_g, u["ss"], 1, 1)
                new_d_state = total(
                    new_d_state,
                    dot3(u["qs"], d_os_g, 0, 0),
                    dot3(u["ks"], d_es_g, 0, 0),
                )
            d_cum = row_sum(u["q"] * d_q + u["k"] * (d_k_plus - d_k_minus))
            if d_last is not None:
                tail_row = lax.broadcasted_iota(jnp.int32, (chunk, 1), 0) == chunk - 1
                d_cum = d_cum + jnp.where(tail_row, d_last, 0.0)
            d_beta_cols[h, c] = d_beta
            d_cum_cols[h, c] = d_cum
            d_q_parts[c] = d_q
            d_k_parts[c] = d_k_plus + d_k_minus
            d_state = new_d_state
        d_q = jnp.concatenate(d_q_parts, axis=0) * scale
        d_k = jnp.concatenate(d_k_parts, axis=0)
        dact_ref[:, h * DK : (h + 1) * DK] = q_rs[h] * (
            d_q - q_hat[h] * row_sum(q_hat[h] * d_q)
        )
        dact_ref[:, (H + h) * DK : (H + h + 1) * DK] = k_rs[h] * (
            d_k - k_hat[h] * row_sum(k_hat[h] * d_k)
        )

    lane = lax.broadcasted_iota(jnp.int32, (chunk, lanes), 1)
    d_gate_parts = []
    d_dlog = None
    for c in range(chunks):
        span = slice(c * chunk, (c + 1) * chunk)
        d_cum = jnp.zeros((chunk, lanes), f32)
        d_beta = jnp.zeros((chunk, lanes), f32)
        for h in range(H):
            d_cum = jnp.where(lane == H + h, d_cum_cols[h, c], d_cum)
            d_beta = jnp.where(lane == h, d_beta_cols[h, c], d_beta)
        d_log = exact_sum(d_cum, 0)
        d_dlog = total(d_dlog, col_sum(d_log * log_decay[span]))
        sig = gate_sig[span]
        d_gate_parts.append(d_beta * sig * (1.0 - sig) + d_log * decay_rate * sig)
    keep(ddlog_ref, d_dlog)
    d_gate = jnp.concatenate(d_gate_parts, axis=0)
    d_gate_s = split(d_gate)
    keep(dbw_ref, dot3(normed_s, d_gate_s, 0, 0))

    d_taps = []
    for at in range(0, channels, DK):
        conv = conv_ref[:, at : at + DK]
        sig = sigmoid(conv)
        d_conv = dact_ref[:, at : at + DK] * (sig * (1.0 + conv * (1.0 - sig)))
        piece = proj_ref[:, at : at + DK]
        d_piece = None
        tap_rows = []
        for tap in range(CONV):
            by = CONV - 1 - tap
            tap_rows.append(col_sum(d_conv * shifted(piece, by)))
            d_piece = total(
                d_piece, taps_ref[tap : tap + 1, at : at + DK] * shifted(d_conv, -by)
            )
        dproj_ref[:, at : at + DK] = d_piece.astype(bf16)
        d_taps.append(jnp.concatenate(tap_rows, axis=0))
    keep(dtaps_ref, jnp.concatenate(d_taps, axis=1))

    keep(gin_ref, dot(normed_bf, dproj_ref[...], 0, 0))
    d_normed = dot(dproj_ref[...], win_ref[...], 1, 1) + dot3(d_gate_s, bw_s, 1, 1)
    keep(dgain_ref, col_sum(d_normed * x_hat))
    d_hat = d_normed * gain
    d_x = x_scale * (d_hat - x_hat * jnp.mean(x_hat * d_hat, axis=1, keepdims=True))
    xgrad_ref[0] = upstream.astype(f32) + d_x


def local_step(
    seq_valid, block_input, cotangent, in_full, out_full, gain, bw, taps, dlog, ogain
):
    seqs, length, width = block_input.shape
    proj_cols = in_full.shape[1]
    mixed_cols = out_full.shape[0]
    channels = taps.shape[1]
    f32 = jnp.float32
    token = pl.BlockSpec((1, length, width), lambda i: (i, 0, 0))

    def whole(shape):
        return pl.BlockSpec(shape, lambda i: (0, 0))

    sums = [
        in_full.shape,
        out_full.shape,
        gain.shape,
        bw.shape,
        taps.shape,
        dlog.shape,
        ogain.shape,
    ]
    return pl.pallas_call(
        functools.partial(local_kernel, seqs=seqs),
        grid=(seqs,),
        in_specs=[pl.BlockSpec(memory_space=pltpu.SMEM), token, token]
        + [whole(shape) for shape in sums],
        out_specs=[token, token] + [whole(shape) for shape in sums],
        out_shape=[jax.ShapeDtypeStruct(block_input.shape, f32)] * 2
        + [jax.ShapeDtypeStruct(shape, f32) for shape in sums],
        scratch_shapes=[
            pltpu.VMEM((length, proj_cols), f32),
            pltpu.VMEM((length, channels), f32),
            pltpu.VMEM((length, mixed_cols), jnp.bfloat16),
            pltpu.VMEM((length, proj_cols), jnp.bfloat16),
            pltpu.VMEM((length, channels), f32),
        ],
        compiler_params=pltpu.CompilerParams(
            dimension_semantics=("arbitrary",), vmem_limit_bytes=60 * 1024 * 1024
        ),
        name="local_step",
    )(seq_valid, block_input, cotangent, in_full, out_full, gain, bw, taps, dlog, ogain)


def adamw(weight, grad, moment, second):
    moment_new = BETA_ONE * moment + (1.0 - BETA_ONE) * grad
    second_new = BETA_TWO * second + (1.0 - BETA_TWO) * grad * grad
    update = (
        moment_new
        / (1.0 - BETA_ONE**STEP)
        / (jnp.sqrt(second_new / (1.0 - BETA_TWO**STEP)) + ADAM_EPS)
    )
    return (weight - LEARN_RATE * (update + WEIGHT_DECAY * weight), moment_new, second_new)


def on_device(
    block_input,
    cotangent,
    seq_valid,
    in_weight,
    out_weight,
    small_params,
    in_moment,
    in_second,
    out_moment,
    out_second,
    small_moment,
    small_second,
):
    gain_in, beta_weight, conv_taps, decay_log, out_gain = split_small(small_params)
    in_full = lax.all_gather(in_weight.astype(jnp.bfloat16), "fsdp", axis=0, tiled=True)
    out_full = lax.all_gather(out_weight.astype(jnp.bfloat16), "fsdp", axis=0, tiled=True)
    lanes = 128
    (
        block_output,
        input_grad,
        in_local,
        out_local,
        d_gain_in,
        d_beta_weight,
        d_conv,
        d_decay,
        d_gain_out,
    ) = local_step(
        seq_valid,
        block_input,
        cotangent,
        in_full,
        out_full,
        gain_in[None],
        jnp.pad(beta_weight, ((0, 0), (0, lanes - 2 * H))),
        conv_taps,
        jnp.pad(decay_log[None], ((0, 0), (H, lanes - 2 * H))),
        out_gain[None],
    )
    in_owned = lax.psum_scatter(
        in_local, "fsdp", scatter_dimension=0, tiled=True
    )
    out_owned = lax.psum_scatter(
        out_local, "fsdp", scatter_dimension=0, tiled=True
    )
    in_grad, out_grad = lax.psum((in_owned, out_owned), "rep")
    small_local = jnp.concatenate(
        [
            d_gain_in[0],
            d_beta_weight[:, : 2 * H].reshape(-1),
            d_conv.reshape(-1),
            d_decay[0, H : 2 * H],
            d_gain_out[0],
        ]
    )
    small_grad = lax.psum(small_local, ("rep", "fsdp"))
    new_in, in_m, in_v = adamw(in_weight, in_grad, in_moment, in_second)
    new_out, out_m, out_v = adamw(out_weight, out_grad, out_moment, out_second)
    new_small, small_m, small_v = adamw(small_params, small_grad, small_moment, small_second)
    return (
        block_output,
        input_grad,
        in_grad,
        out_grad,
        small_grad,
        new_in,
        new_out,
        new_small,
        in_m,
        in_v,
        out_m,
        out_v,
        small_m,
        small_v,
    )


def solution(mesh):
    in_specs = (
        P(("rep", "fsdp"), None, None),
        P(("rep", "fsdp"), None, None),
        P(("rep", "fsdp")),
        P("fsdp", None),
        P("fsdp", None),
        P(),
        P("fsdp", None),
        P("fsdp", None),
        P("fsdp", None),
        P("fsdp", None),
        P(),
        P(),
    )
    out_specs = (
        P(("rep", "fsdp"), None, None),
        P(("rep", "fsdp"), None, None),
        P("fsdp", None),
        P("fsdp", None),
        P(),
        P("fsdp", None),
        P("fsdp", None),
        P(),
        P("fsdp", None),
        P("fsdp", None),
        P("fsdp", None),
        P("fsdp", None),
        P(),
        P(),
    )
    return jax.shard_map(
        on_device, mesh=mesh, in_specs=in_specs, out_specs=out_specs, check_vma=False
    )
```

time: 578 us -> 236 us (0.41)
  other arithmetic: 204 us -> 8.5 us
  matrix products: 116 us -> 0 us
  local copies, waits for them, and re-layouts: 75.1 us -> 8.9 us
  waiting for transfers between devices: 94.2 us -> 121 us
  Pallas kernels: 0 us -> 16.3 us
    another operation x73 -> x0, other arithmetic: 139 us -> none  [the longest x44 126 us: tri_solve(): lax.linalg.triangular_solve(matrix, right, left_side=True, lower=True, un...]
    dot_general x89 -> x0, matrix products: 87.2 us -> none  [the longest x12 13.4 us: one_block(): jnp.einsum('hij,hjv->hiv', scores, delta_residual, precision=HIGHEST_ACCU...]
    reduce_scatter x2, waiting for transfers between devices: 21.4 us -> 86.7 us  [the longest x1 61.2 us: on_device(): lax.psum_scatter(in_local, 'fsdp', scatter_dimension=0, tiled=True)]
    psum x1, waiting for transfers between devices: 56.1 us -> 18.3 us  [on_device(): in_grad, out_grad = lax.psum((in_owned, out_owned), 'rep')]
    another operation x24 -> x0, matrix products: 29.1 us -> none  [tri_solve(): lax.linalg.triangular_solve(matrix, right, left_side=True, lower=True, un...]
    reduce_sum x28 -> x0, other arithmetic: 23.2 us -> none  [the longest x4 4.03 us: one_block(): corrected_value = tri_solve(system, beta_rows[..., None] * value_rows)]
    dynamic_update_slice x20 -> x0, other arithmetic: 18.6 us -> none  [blockwise(): _, outputs = lax.scan(one_block, initial, grouped)]
    pallas_call x0 -> x1, Pallas kernels: none -> 16.3 us  [local_step(): pl.pallas_call(functools.partial(local_kernel, seqs=seqs), grid=(seqs,),...]
  transfers between devices with their start and end apart: 4 -> 4, of which waited for: 3 -> 4; matrix products, arithmetic and copies ran while one was open for 5% -> 4% of each run, Pallas kernels for 0% -> 0%
where the time goes in v1:
time: 236 us; the launch traced here: 235 us
  waiting for transfers between devices  121 us (51%)
  blocking collectives  65.3 us (28%)
  Pallas kernels  16.3 us (7%)
  between operations  14.6 us (6%)
  local copies, waits for them, and re-layouts  8.9 us (4%)
  other arithmetic  8.5 us (4%)
    reduce_scatter x1, waiting for transfers between devices, on_device(): lax.psum_scatter(in_local, 'fsdp', scatter_dimension=0, tiled=True)  61.2 us
    psum x1, blocking collectives, on_device(): small_grad = lax.psum(small_local, ('rep', 'fsdp'))  40.4 us
    reduce_scatter x1, waiting for transfers between devices, on_device(): lax.psum_scatter(out_local, 'fsdp', scatter_dimension=0, tiled=True)  25.5 us
    all_gather x1, blocking collectives, on_device(): lax.all_gather(out_weight.astype(jnp.bfloat16), 'fsdp', axis=0, tiled=True)  24.9 us
    psum x1, waiting for transfers between devices, on_device(): in_grad, out_grad = lax.psum((in_owned, out_owned), 'rep')  18.3 us
    pallas_call x1, Pallas kernels, local_step(): pl.pallas_call(functools.partial(local_kernel, seqs=seqs), grid=(seqs,),...  16.3 us
    all_gather x1, waiting for transfers between devices, on_device(): lax.all_gather(in_weight.astype(jnp.bfloat16), 'fsdp', axis=0, tiled=True)  15.7 us
    sub x3, other arithmetic, adamw(): weight - LEARN_RATE * (update + WEIGHT_DECAY * weight)  5.62 us
  transfers between devices with their start and end apart: 4, of which 4 were waited for; matrix products, arithmetic and copies ran while one was open for 4% of the time, Pallas kernels for 0%

profile of v1, /device:TPU:0, one launch (start us, length us, event | category | flops | bytes accessed | tf_op | source)
XLA Modules:
  0.0 235.3 jit_solution(6201970716471341971)
XLA Ops:
  7.2 0.0 all-gather.2.cloned.1.call-start
  7.2 1.9 convert_element_type.10
  9.1 0.0 all-gather.2.cloned.1.call-update
  9.2 0.0 reduce-scatter.5.cloned.1.call-start
  9.2 1.3 slice.25
  10.5 1.3 slice.21
  11.8 0.7 slice.22
  12.5 0.7 slice.23
  13.9 0.6 reshape.41.taps_ref
  14.5 1.0 convert_element_type.11
  15.5 0.3 reshape.40
  15.8 0.7 slice_bitcast_fusion.1
  16.4 0.6 pad.9.dlog_ref
  17.0 0.7 pad.8.bw_ref
  17.8 24.9 %all_gather.7.wout_ref = bf16[512,512]{1,0:T(8,128)(2,1)} all-gather(bf16[128,512]{1,0:T(8,128)(2,1)S(1)} %convert_element_type.11), channel_id=1, replica_groups=mesh['rep'=8,'fsdp'=4] {'fsdp'}, dimensions={0}, use_global_device_ids=true | all-gather | bytes 655360 | tf_op jit(solution)/shard_map/all_gather | solution.py:474
  42.7 15.7 %all-gather.2.cloned.1.call-done.win_ref = bf16[512,1536]{1,0:T(8,128)(2,1)} async-done(((bf16[128,1536]{1,0:T(8,128)(2,1)}), bf16[512,1536]{1,0:T(8,128)(2,1)}) %all-gather.2.cloned.1.call-update) | async-done | bytes 1572880 | tf_op jit(solution)/shard_map/all_gather | solution.py:473
  58.3 16.3 %local_step.1 = (f32[1,256,512]{2,1,0:T(8,128)}, f32[1,256,512]{2,1,0:T(8,128)}, f32[512,1536]{1,0:T(8,128)}, f32[512,512]{1,0:T(8,128)}, f32[1,512]{1,0:T(1,128...) custom-call(s32[1]{0:T(128)S(6)} %copy.31.flag_ref, ...), custom_call_target="tpu_custom_call" | custom-call | tf_op jit(solution)/shard_map/local_step/pallas_call | solution.py:425
  74.6 0.0 copy-start.13
  74.7 0.0 copy-start.16
  74.7 0.0 copy-start.14
  74.7 0.0 copy-start.15
  74.7 0.0 copy-start.10
  74.7 0.0 copy-start.11
  74.7 0.0 copy-start.12
  74.7 0.0 copy-start.2
  74.7 0.0 copy-start.6
  74.8 0.0 copy-start.7
  74.8 0.0 reduce-scatter.5.cloned.1.call-update
  74.8 0.0 reduce-scatter.3.cloned.1.call-start
  74.8 0.0 copy-start
  74.9 0.0 copy-start.4
  74.9 0.0 copy-start.5
  74.9 0.6 reduce-scatter.3.cloned.1.call-update
  75.5 0.0 all-reduce.5.cloned.1.call-start
  75.6 25.5 %reduce-scatter.5.cloned.1.call-done = f32[128,512]{1,0:T(8,128)} async-done(((f32[512,512]{1,0:T(8,128)}), f32[128,512]{1,0:T(8,128)}) %reduce-scatter.5.cloned.1.call-update) | async-done | bytes 262160 | tf_op jit(solution)/shard_map/reduce_scatter | solution.py:501
  101.1 61.2 %reduce-scatter.3.cloned.1.call-done = f32[128,1536]{1,0:T(8,128)} async-done(((f32[512,1536]{1,0:T(8,128)}), f32[128,1536]{1,0:T(8,128)}) %reduce-scatter.3.cloned.1.call-update) | async-done | bytes 786448 | tf_op jit(solution)/shard_map/reduce_scatter | solution.py:498
  162.3 0.0 all-reduce.5.cloned.1.call-update
  162.3 0.0 copy-done.8
  162.4 0.2 reshape.42
  162.5 0.0 copy-done.13
  162.5 0.0 copy-done.16
  162.5 0.1 slice_bitcast_fusion
  162.6 0.0 copy-done.14
  162.6 0.0 copy-done.15
  162.6 0.1 concatenate.3
  162.7 40.4 %psum.23 = f32[6914]{0:T(1024)S(1)} all-reduce(f32[6914]{0:T(1024)S(1)} %concatenate.3), channel_id=1, replica_groups=mesh['rep'=8,'fsdp'=4] {'rep','fsdp'}, use_global_device_ids=true, to_apply=%region_4.5 | all-reduce | flops 6914 | bytes 55312 | tf_op jit(solution)/shard_map/psum | solution.py:514
  203.1 0.0 copy-done.10
  203.1 0.0 copy-done.11
  203.2 0.0 copy-done.12
  203.2 0.0 copy-start.9
  203.2 0.6 multiply_subtract_fusion.2
  203.8 18.3 %all-reduce.5.cloned.1.call-done = (f32[128,1536]{1,0:T(8,128)}, f32[128,512]{1,0:T(8,128)}) async-done(((f32[128,1536]{1,0:T(8,128)}, f32[128,512]{1,0:T(8,128)}), (f32[128,1536]{1,0:T(8,128)}, f32[128,512]{1,0:T(8,128)})) %all-reduce.5.cloned.1.call-update) | async-done | bytes 1048592 | tf_op jit(solution)/shard_map/psum | solution.py:504
  222.2 0.0 copy-done.2
  222.2 0.0 copy-done.6
  222.2 0.0 copy-done.7
  222.2 2.0 multiply_subtract_fusion.1
  224.1 0.0 copy-done
  224.1 0.0 copy-done.4
  224.1 0.0 copy-done.5
  224.1 0.0 copy-start.3
  224.2 3.0 %multiply_subtract_fusion = (f32[128,1536]{1,0:T(8,128)}, f32[128,1536]{1,0:T(8,128)}, f32[128,1536]{1,0:T(8,128)}) fusion(f32[128,1536]{1,0:T(8,128)S(1)} %copy-done, f32[128,1536]{1,0:T(8,128)} %get-tuple-element.45, f32[128,1536]{1,0:T(8,128)S(1)} %copy-done.4, f32[128,1536]{1,0:T(8,128)S(1)} %copy-done.5), kind=kLoop, calls=%fused_computation.2 | loop fusion | flops 2949120 | bytes 5505024 | tf_op jit(solution)/shard_map/sub | solution.py:455
  227.2 0.0 copy-done.9
  227.2 0.9 copy.32
  228.1 0.7 copy.33
  (5 shorter events, 0.0 us)
Async XLA Ops:
  7.2 51.2 %all-gather.2.cloned.1.call-start = ((), (), s32[]{:S(2)}) async-start(), calls=%async_computation.2 | async-start | bytes 1966080 | tf_op jit(solution)/shard_map/all_gather | solution.py:473
  9.2 91.9 %reduce-scatter.5.cloned.1.call-start = ((), (), s32[]{:S(2)}) async-start(), calls=%async_computation.4 | async-start | bytes 1310720 | tf_op jit(solution)/shard_map/reduce_scatter | solution.py:501
  74.6 87.7 %copy-start.8 = (f32[512,128]{1,0:T(8,128)S(1)}, f32[512,128]{1,0:T(8,128)}, u32[]{:S(2)}) copy-start(f32[512,128]{1,0:T(8,128)} %get-tuple-element.28) | copy-start | bytes 786436
  74.6 87.9 %copy-start.13 = (f32[4,1024]{1,0:T(4,128)S(1)}, f32[4,1024]{1,0:T(4,128)}, u32[]{:S(2)}) copy-start(f32[4,1024]{1,0:T(4,128)} %get-tuple-element.29) | copy-start | bytes 49156
  74.7 87.9 %copy-start.16 = (f32[1,128]{1,0:T(1,128)S(1)}, f32[1,128]{1,0:T(1,128)}, u32[]{:S(2)}) copy-start(f32[1,128]{1,0:T(1,128)} %get-tuple-element.30) | copy-start | bytes 1540
  74.7 87.9 %copy-start.14 = (f32[1,512]{1,0:T(1,128)S(1)}, f32[1,512]{1,0:T(1,128)}, u32[]{:S(2)}) copy-start(f32[1,512]{1,0:T(1,128)} %get-tuple-element.27) | copy-start | bytes 6148
  74.7 87.9 %copy-start.15 = (f32[1,256]{1,0:T(1,128)S(1)}, f32[1,256]{1,0:T(1,128)}, u32[]{:S(2)}) copy-start(f32[1,256]{1,0:T(1,128)} %get-tuple-element.31) | copy-start | bytes 3076
  74.7 128.4 %copy-start.10 = (f32[6914]{0:T(1024)S(1)}, f32[6914]{0:T(1024)}, u32[]{:S(2)}) copy-start(f32[6914]{0:T(1024)} %param.17) | copy-start | bytes 82972
  74.7 128.4 %copy-start.11 = (f32[6914]{0:T(1024)S(1)}, f32[6914]{0:T(1024)}, u32[]{:S(2)}) copy-start(f32[6914]{0:T(1024)} %param.22) | copy-start | bytes 82972
  74.7 128.4 %copy-start.12 = (f32[6914]{0:T(1024)S(1)}, f32[6914]{0:T(1024)}, u32[]{:S(2)}) copy-start(f32[6914]{0:T(1024)} %param.23) | copy-start | bytes 82972
  74.7 147.4 %copy-start.2 = (f32[128,512]{1,0:T(8,128)S(1)}, f32[128,512]{1,0:T(8,128)}, u32[]{:S(2)}) copy-start(f32[128,512]{1,0:T(8,128)} %param.16) | copy-start | bytes 786436
  74.7 147.4 %copy-start.6 = (f32[128,512]{1,0:T(8,128)S(1)}, f32[128,512]{1,0:T(8,128)}, u32[]{:S(2)}) copy-start(f32[128,512]{1,0:T(8,128)} %param.20) | copy-start | bytes 786436
  74.8 147.4 %copy-start.7 = (f32[128,512]{1,0:T(8,128)S(1)}, f32[128,512]{1,0:T(8,128)}, u32[]{:S(2)}) copy-start(f32[128,512]{1,0:T(8,128)} %param.21) | copy-start | bytes 786436
  74.8 87.5 %reduce-scatter.3.cloned.1.call-start = ((), (), s32[]{:S(2)}) async-start(), calls=%async_computation.3 | async-start | bytes 3932160 | tf_op jit(solution)/shard_map/reduce_scatter | solution.py:498
  74.8 149.3 %copy-start = (f32[128,1536]{1,0:T(8,128)S(1)}, f32[128,1536]{1,0:T(8,128)}, u32[]{:S(2)}) copy-start(f32[128,1536]{1,0:T(8,128)} %param.15) | copy-start | bytes 2359300
  74.9 149.3 %copy-start.4 = (f32[128,1536]{1,0:T(8,128)S(1)}, f32[128,1536]{1,0:T(8,128)}, u32[]{:S(2)}) copy-start(f32[128,1536]{1,0:T(8,128)} %param.18) | copy-start | bytes 2359300
  74.9 149.3 %copy-start.5 = (f32[128,1536]{1,0:T(8,128)S(1)}, f32[128,1536]{1,0:T(8,128)}, u32[]{:S(2)}) copy-start(f32[128,1536]{1,0:T(8,128)} %param.19) | copy-start | bytes 2359300
  75.5 146.6 %all-reduce.5.cloned.1.call-start = ((), (), s32[]{:S(2)}) async-start(), calls=%async_computation.5 | async-start | bytes 2097152 | tf_op jit(solution)/shard_map/psum | solution.py:504
  203.2 24.0 %copy-start.9 = (f32[6914]{0:T(1024)}, f32[6914]{0:T(1024)S(1)}, u32[]{:S(2)}) copy-start(f32[6914]{0:T(1024)S(1)} %psum.23) | copy-start | bytes 82972
  224.1 3.1 %copy-start.1 = (f32[128,1536]{1,0:T(8,128)S(1)}, f32[128,1536]{1,0:T(8,128)}, u32[]{:S(2)}) copy-start(f32[128,1536]{1,0:T(8,128)} %get-tuple-element.45) | copy-start | bytes 2359300
  224.1 3.9 %copy-start.3 = (f32[128,512]{1,0:T(8,128)S(1)}, f32[128,512]{1,0:T(8,128)}, u32[]{:S(2)}) copy-start(f32[128,512]{1,0:T(8,128)} %get-tuple-element.46) | copy-start | bytes 786436
Sparse Core Ops, SparseCore 0:
  10.1 48.1 all-gather.1
  74.9 26.1 reduce-scatter.4
  103.4 58.8 reduce-scatter.2
  165.4 56.7 all-reduce.4

commit v2 on v1

--- a/solution.py
+++ b/solution.py
@@ -13,6 +13,8 @@
 DV = 256
 CONV = 4
 CHUNK = 128
+GROUPS = 4
+MESH = pl.DeviceIdType.MESH
 STEP = 3
 
 
@@ -98,8 +100,7 @@
     flag_ref,
     x_ref,
     cot_ref,
-    win_ref,
-    wout_ref,
+    blocks_ref,
     gain_ref,
     bw_ref,
     taps_ref,
@@ -107,8 +108,7 @@
     ogain_ref,
     out_ref,
     xgrad_ref,
-    gin_ref,
-    gout_ref,
+    grad_ref,
     dgain_ref,
     dbw_ref,
     dtaps_ref,
@@ -119,6 +119,8 @@
     mixed_ref,
     dproj_ref,
     dact_ref,
+    win_ref,
+    wout_ref,
     *,
     seqs,
 ):
@@ -141,6 +143,22 @@
             @pl.when(pl.program_id(0) > 0)
             def _():
                 ref[...] = ref[...] + value
+
+    shards, col_blocks, shard_rows, block = blocks_ref.shape
+    in_blocks = win_ref.shape[1] // block
+    out_blocks = wout_ref.shape[1] // block
+    for s in range(shards):
+        here = slice(s * shard_rows, (s + 1) * shard_rows)
+        for b in range(in_blocks):
+            win_ref[here, b * block : (b + 1) * block] = blocks_ref[s, b]
+        for b in range(out_blocks):
+            wout_ref[here, b * block : (b + 1) * block] = blocks_ref[s, in_blocks + b]
+
+    def keep_blocks(value, first):
+        for s in range(shards):
+            here = slice(s * shard_rows, (s + 1) * shard_rows)
+            for b in range(value.shape[1] // block):
+                keep(grad_ref.at[s, first + b], value[here, b * block : (b + 1) * block])
 
     gain = gain_ref[...]
     x = x_ref[0].astype(f32)
@@ -288,7 +306,7 @@
             o_grads[h, c] = d_o[c * chunk : (c + 1) * chunk]
     keep(dogain_ref, d_ogain)
     out_ref[0] = x + dot(mixed_ref[...], wout_ref[...])
-    keep(gout_ref, dot(mixed_ref[...], upstream, 0, 0))
+    keep_blocks(dot(mixed_ref[...], upstream, 0, 0), in_blocks)
 
     d_beta_cols = {}
     d_cum_cols = {}
@@ -392,7 +410,7 @@
         d_taps.append(jnp.concatenate(tap_rows, axis=0))
     keep(dtaps_ref, jnp.concatenate(d_taps, axis=1))
 
-    keep(gin_ref, dot(normed_bf, dproj_ref[...], 0, 0))
+    keep_blocks(dot(normed_bf, dproj_ref[...], 0, 0), 0)
     d_normed = dot(dproj_ref[...], win_ref[...], 1, 1) + dot3(d_gate_s, bw_s, 1, 1)
     keep(dgain_ref, col_sum(d_normed * x_hat))
     d_hat = d_normed * gain
@@ -401,27 +419,19 @@
 
 
 def local_step(
-    seq_valid, block_input, cotangent, in_full, out_full, gain, bw, taps, dlog, ogain
+    seq_valid, block_input, cotangent, blocks, gain, bw, taps, dlog, ogain, in_cols
 ):
     seqs, length, width = block_input.shape
-    proj_cols = in_full.shape[1]
-    mixed_cols = out_full.shape[0]
+    shards, col_blocks, shard_rows, block = blocks.shape
+    out_cols = col_blocks * block - in_cols
     channels = taps.shape[1]
     f32 = jnp.float32
     token = pl.BlockSpec((1, length, width), lambda i: (i, 0, 0))
 
     def whole(shape):
-        return pl.BlockSpec(shape, lambda i: (0, 0))
-
-    sums = [
-        in_full.shape,
-        out_full.shape,
-        gain.shape,
-        bw.shape,
-        taps.shape,
-        dlog.shape,
-        ogain.shape,
-    ]
+        return pl.BlockSpec(shape, lambda i: (0,) * len(shape))
+
+    sums = [blocks.shape, gain.shape, bw.shape, taps.shape, dlog.shape, ogain.shape]
     return pl.pallas_call(
         functools.partial(local_kernel, seqs=seqs),
         grid=(seqs,),
@@ -431,17 +441,288 @@
         out_shape=[jax.ShapeDtypeStruct(block_input.shape, f32)] * 2
         + [jax.ShapeDtypeStruct(shape, f32) for shape in sums],
         scratch_shapes=[
-            pltpu.VMEM((length, proj_cols), f32),
+            pltpu.VMEM((length, in_cols), f32),
             pltpu.VMEM((length, channels), f32),
-            pltpu.VMEM((length, mixed_cols), jnp.bfloat16),
-            pltpu.VMEM((length, proj_cols), jnp.bfloat16),
+            pltpu.VMEM((length, H * DV), jnp.bfloat16),
+            pltpu.VMEM((length, in_cols), jnp.bfloat16),
             pltpu.VMEM((length, channels), f32),
+            pltpu.VMEM((shards * shard_rows, in_cols), jnp.bfloat16),
+            pltpu.VMEM((shards * shard_rows, out_cols), jnp.bfloat16),
         ],
         compiler_params=pltpu.CompilerParams(
             dimension_semantics=("arbitrary",), vmem_limit_bytes=60 * 1024 * 1024
         ),
         name="local_step",
-    )(seq_valid, block_input, cotangent, in_full, out_full, gain, bw, taps, dlog, ogain)
+    )(seq_valid, block_input, cotangent, blocks, gain, bw, taps, dlog, ogain)
+
+
+def greet(replicas, shards):
+    rep, shard = lax.axis_index("rep"), lax.axis_index("fsdp")
+    barrier = pltpu.get_barrier_semaphore()
+    bits = replicas.bit_length() - 1
+    for bit in range(bits):
+        pl.semaphore_signal(
+            barrier, inc=1, device_id=(flip(rep, bit), shard), device_id_type=MESH
+        )
+    for step in range(1, shards):
+        pl.semaphore_signal(
+            barrier,
+            inc=1,
+            device_id=(rep, lax.rem(shard + step, shards)),
+            device_id_type=MESH,
+        )
+    pl.semaphore_wait(barrier, bits + shards - 1)
+
+
+def bit_of(rep, bit):
+    return lax.rem(rep // (1 << bit), 2)
+
+
+def flip(rep, bit):
+    return rep + (1 << bit) * (1 - 2 * bit_of(rep, bit))
+
+
+def bit_orders(replicas):
+    bits = list(range(replicas.bit_length() - 1))
+    return [bits, bits[:1] + bits[1:][::-1]]
+
+
+def aligned(offset, size):
+    return pl.ds(pl.multiple_of(offset, size), size)
+
+
+class Copies:
+    def __init__(self, send_sems, recv_sems):
+        self.send_sems, self.recv_sems, self.started = send_sems, recv_sems, []
+
+    def start(self, src, dst, rep, shard):
+        at = len(self.started)
+        copy = pltpu.make_async_remote_copy(
+            src_ref=src,
+            dst_ref=dst,
+            send_sem=self.send_sems.at[at],
+            recv_sem=self.recv_sems.at[at],
+            device_id=(rep, shard),
+            device_id_type=MESH,
+        )
+        copy.start()
+        self.started.append(copy)
+        return copy
+
+    def finish(self):
+        for copy in self.started:
+            copy.wait_send()
+
+
+def gather_kernel(replicas, shards, win_ref, wout_ref, full_ref, mine_ref, send_sems, recv_sems):
+    rep, shard = lax.axis_index("rep"), lax.axis_index("fsdp")
+    rows, block = win_ref.shape[0], full_ref.shape[-1]
+    at = 0
+    for ref in (win_ref, wout_ref):
+        for b in range(ref.shape[1] // block):
+            value = ref[:, b * block : (b + 1) * block].astype(jnp.bfloat16)
+            mine_ref[at : at + rows, :] = value
+            at += rows
+    full_ref[shard] = mine_ref[...]
+    greet(replicas, shards)
+    copies = Copies(send_sems, recv_sems)
+    orders = bit_orders(replicas)
+    span = mine_ref.shape[0] // len(orders)
+    state = []
+    for g, order in enumerate(orders):
+        size, base = span, g * span
+        for bit in order:
+            size //= 2
+            base = base + bit_of(rep, bit) * size
+        pending = []
+        for step in range(1, shards):
+            pending.append(
+                copies.start(
+                    mine_ref.at[aligned(base, size), :],
+                    full_ref.at[shard, aligned(base, size), :],
+                    rep,
+                    lax.rem(shard + step, shards),
+                )
+            )
+        state.append([base, size, pending])
+    for level in range(len(orders[0])):
+        for g, order in enumerate(orders):
+            base, size, pending = state[g]
+            for copy in pending:
+                copy.wait_recv()
+            bit = order[len(order) - 1 - level]
+            here = full_ref.at[:, aligned(base, size), :]
+            pending = [copies.start(here, here, flip(rep, bit), shard)]
+            state[g] = [base - bit_of(rep, bit) * size, 2 * size, pending]
+    for _, _, pending in state:
+        for copy in pending:
+            copy.wait_recv()
+    copies.finish()
+
+
+def gather_weights(replicas, shards, in_weight, out_weight):
+    rows, block = in_weight.shape[0], 128
+    total_rows = rows * (in_weight.shape[1] + out_weight.shape[1]) // block
+    bits = replicas.bit_length() - 1
+    count = 2 * (bits + shards - 1)
+    return pl.pallas_call(
+        functools.partial(gather_kernel, replicas, shards),
+        in_specs=[pl.BlockSpec(memory_space=pltpu.VMEM)] * 2,
+        out_specs=pl.BlockSpec(memory_space=pltpu.VMEM),
+        out_shape=jax.ShapeDtypeStruct((shards, total_rows, block), jnp.bfloat16),
+        scratch_shapes=[
+            pltpu.VMEM((total_rows, block), jnp.bfloat16),
+            pltpu.SemaphoreType.DMA((count,)),
+            pltpu.SemaphoreType.DMA((count,)),
+        ],
+        compiler_params=pltpu.CompilerParams(
+            collective_id=0, has_side_effects=True, vmem_limit_bytes=24 * 1024 * 1024
+        ),
+        name="gather_weights",
+    )(in_weight, out_weight)
+
+
+def reduce_kernel(replicas, shards, grad_ref, small_ref, out_ref, small_out_ref, *scratch):
+    rep, shard = lax.axis_index("rep"), lax.axis_index("fsdp")
+    send_sems, recv_sems = scratch[-2:]
+    orders = bit_orders(replicas)
+    bits = len(orders[0])
+    copies = Copies(send_sems, recv_sems)
+    greet(replicas, shards)
+    span = grad_ref.shape[1] // GROUPS
+    groups = []
+    for g in range(GROUPS + 1):
+        bufs = scratch[g * (bits + 1) : (g + 1) * (bits + 1)]
+        if g < GROUPS:
+            groups.append([grad_ref, out_ref, g * span, span, orders[g % 2], bufs])
+        else:
+            groups.append(
+                [small_ref, small_out_ref, 0, small_ref.shape[1], orders[0], bufs]
+            )
+
+    def halve(group, level):
+        cur, _, base, size, order, bufs = group
+        half = size // 2
+        mine = bit_of(rep, order[level])
+        there = base + (1 - mine) * half
+        copy = copies.start(
+            cur.at[:, aligned(there, half), :], bufs[level], flip(rep, order[level]), shard
+        )
+        return copy, base + mine * half, half
+
+    live = [halve(group, 0) for group in groups]
+    for level in range(bits):
+        for g, group in enumerate(groups):
+            copy, mine, half = live[g]
+            cur, bufs = group[0], group[5]
+            copy.wait_recv()
+            bufs[level][...] = bufs[level][...] + cur[:, aligned(mine, half), :]
+            group[0], group[2], group[3] = bufs[level], 0, half
+            if level + 1 < bits:
+                live[g] = halve(group, level + 1)
+            else:
+                pending = []
+                for step in range(1, shards):
+                    to = lax.rem(shard + step, shards)
+                    if g < GROUPS:
+                        src, slot = group[0].at[to], bufs[bits].at[step - 1]
+                    else:
+                        src, slot = group[0].at[0], bufs[bits].at[shard]
+                    pending.append(copies.start(src, slot, rep, to))
+                live[g] = pending
+    spread = []
+    for g, group in enumerate(groups):
+        cur, out, _, size, order, bufs = group
+        base = g * span if g < GROUPS else 0
+        full = span if g < GROUPS else small_ref.shape[1]
+        for bit in order:
+            full //= 2
+            base = base + bit_of(rep, bit) * full
+        if g == GROUPS:
+            bufs[bits][shard] = cur[0]
+        for copy in live[g]:
+            copy.wait_recv()
+        if g < GROUPS:
+            value = cur[shard]
+            for step in range(1, shards):
+                value = value + bufs[bits][step - 1]
+        else:
+            value = bufs[bits][0]
+            for s in range(1, shards):
+                value = value + bufs[bits][s]
+        out[aligned(base, size), :] = value
+        spread.append([base, size, None])
+        start_spread(copies, out, spread[g], order[-1], rep, shard)
+    for level in range(1, bits + 1):
+        for g, group in enumerate(groups):
+            spread[g][2].wait_recv()
+            if level < bits:
+                start_spread(
+                    copies, group[1], spread[g], group[4][bits - 1 - level], rep, shard
+                )
+    copies.finish()
+
+
+def start_spread(copies, out, state, bit, rep, shard):
+    base, size, _ = state
+    here = out.at[aligned(base, size), :]
+    copy = copies.start(here, here, flip(rep, bit), shard)
+    state[:] = [base - bit_of(rep, bit) * size, 2 * size, copy]
+
+
+def reduce_grads(replicas, shards, grads, small):
+    rows, block = grads.shape[1:]
+    bits = replicas.bit_length() - 1
+    scratch = []
+    for g in range(GROUPS + 1):
+        parts, size = (shards, rows // GROUPS) if g < GROUPS else (1, small.shape[1])
+        for _ in range(bits):
+            size //= 2
+            scratch.append(pltpu.VMEM((parts, size, block), jnp.float32))
+        slots = shards - 1 if g < GROUPS else shards
+        scratch.append(pltpu.VMEM((slots, size, block), jnp.float32))
+    count = (GROUPS + 1) * (2 * bits + shards - 1)
+    return pl.pallas_call(
+        functools.partial(reduce_kernel, replicas, shards),
+        in_specs=[pl.BlockSpec(memory_space=pltpu.VMEM)] * 2,
+        out_specs=[pl.BlockSpec(memory_space=pltpu.VMEM)] * 2,
+        out_shape=[
+            jax.ShapeDtypeStruct((rows, block), jnp.float32),
+            jax.ShapeDtypeStruct(small.shape[1:], jnp.float32),
+        ],
+        scratch_shapes=scratch
+        + [pltpu.SemaphoreType.DMA((count,)), pltpu.SemaphoreType.DMA((count,))],
+        compiler_params=pltpu.CompilerParams(
+            collective_id=1, has_side_effects=True, vmem_limit_bytes=40 * 1024 * 1024
+        ),
+        name="reduce_grads",
+    )(grads, small)
+
+
+def adam_kernel(grad_ref, *refs):
+    rows, block = refs[0].shape[0], grad_ref.shape[1]
+    at = 0
+    for first in (0, 3):
+        weight, moment, second = refs[first : first + 3]
+        outs = refs[6 + 4 * (first // 3) : 10 + 4 * (first // 3)]
+        for b in range(weight.shape[1] // block):
+            cols = slice(b * block, (b + 1) * block)
+            grad = grad_ref[at : at + rows, :]
+            at += rows
+            new = adamw(weight[:, cols], grad, moment[:, cols], second[:, cols])
+            for ref, value in zip(outs, (grad,) + new):
+                ref[:, cols] = value
+
+
+def adam_large(grad, in_state, out_state):
+    shapes = [a.shape for a in (in_state[0],) * 4 + (out_state[0],) * 4]
+    return pl.pallas_call(
+        adam_kernel,
+        in_specs=[pl.BlockSpec(memory_space=pltpu.VMEM)] * 7,
+        out_specs=[pl.BlockSpec(memory_space=pltpu.VMEM)] * 8,
+        out_shape=[jax.ShapeDtypeStruct(shape, jnp.float32) for shape in shapes],
+        name="adam_large",
+    )(grad, *in_state, *out_state)
 
 
 def adamw(weight, grad, moment, second):
@@ -470,14 +751,14 @@
     small_second,
 ):
     gain_in, beta_weight, conv_taps, decay_log, out_gain = split_small(small_params)
-    in_full = lax.all_gather(in_weight.astype(jnp.bfloat16), "fsdp", axis=0, tiled=True)
-    out_full = lax.all_gather(out_weight.astype(jnp.bfloat16), "fsdp", axis=0, tiled=True)
+    replicas, shards = lax.axis_size("rep"), lax.axis_size("fsdp")
+    shard_rows, in_cols = in_weight.shape
+    blocks = gather_weights(replicas, shards, in_weight, out_weight)
     lanes = 128
     (
         block_output,
         input_grad,
-        in_local,
-        out_local,
+        grads,
         d_gain_in,
         d_beta_weight,
         d_conv,
@@ -487,21 +768,14 @@
         seq_valid,
         block_input,
         cotangent,
-        in_full,
-        out_full,
+        blocks.reshape(shards, -1, shard_rows, blocks.shape[-1]),
         gain_in[None],
         jnp.pad(beta_weight, ((0, 0), (0, lanes - 2 * H))),
         conv_taps,
         jnp.pad(decay_log[None], ((0, 0), (H, lanes - 2 * H))),
         out_gain[None],
-    )
-    in_owned = lax.psum_scatter(
-        in_local, "fsdp", scatter_dimension=0, tiled=True
-    )
-    out_owned = lax.psum_scatter(
-        out_local, "fsdp", scatter_dimension=0, tiled=True
-    )
-    in_grad, out_grad = lax.psum((in_owned, out_owned), "rep")
+        in_cols,
+    )
     small_local = jnp.concatenate(
         [
             d_gain_in[0],
@@ -511,9 +785,19 @@
             d_gain_out[0],
         ]
     )
-    small_grad = lax.psum(small_local, ("rep", "fsdp"))
-    new_in, in_m, in_v = adamw(in_weight, in_grad, in_moment, in_second)
-    new_out, out_m, out_v = adamw(out_weight, out_grad, out_moment, out_second)
+    count = small_local.shape[0]
+    unit = 8 * replicas * lanes
+    padded = jnp.pad(small_local, (0, -count % unit))
+    grad, small_sum = reduce_grads(
+        replicas,
+        shards,
+        grads.reshape(shards, -1, lanes),
+        padded.reshape(1, -1, lanes),
+    )
+    small_grad = small_sum.reshape(-1)[:count]
+    in_grad, new_in, in_m, in_v, out_grad, new_out, out_m, out_v = adam_large(
+        grad, (in_weight, in_moment, in_second), (out_weight, out_moment, out_second)
+    )
     new_small, small_m, small_v = adamw(small_params, small_grad, small_moment, small_second)
     return (
         block_output,

time: 236 us -> 107 us (0.45)
  waiting for transfers between devices: 121 us -> 0 us
  Pallas kernels: 16.3 us -> 87.9 us
  blocking collectives: 65.3 us -> 0 us
  between operations: 14.6 us -> 1.35 us
  local copies, waits for them, and re-layouts: 8.9 us -> 16.8 us
  other arithmetic: 8.5 us -> 0.65 us
    reduce_scatter x2 -> x0, waiting for transfers between devices: 86.7 us -> none  [the longest x1 61.2 us: on_device(): lax.psum_scatter(in_local, 'fsdp', scatter_dimension=0, tiled=True)]
    pallas_call x0 -> x3, Pallas kernels: none -> 70.8 us  [the longest x1 41.2 us: reduce_grads(): pl.pallas_call(functools.partial(reduce_kernel, replicas, shards), in_spe...]
    psum x1 -> x0, blocking collectives: 40.4 us -> none  [on_device(): small_grad = lax.psum(small_local, ('rep', 'fsdp'))]
    all_gather x1 -> x0, blocking collectives: 24.9 us -> none  [on_device(): lax.all_gather(out_weight.astype(jnp.bfloat16), 'fsdp', axis=0, tiled=True)]
    psum x1 -> x0, waiting for transfers between devices: 18.3 us -> none  [on_device(): in_grad, out_grad = lax.psum((in_owned, out_owned), 'rep')]
    all_gather x1 -> x0, waiting for transfers between devices: 15.7 us -> none  [on_device(): lax.all_gather(in_weight.astype(jnp.bfloat16), 'fsdp', axis=0, tiled=True)]
    unnamed x37 -> x17, local copies, waits for them, and re-layouts: 1.69 us -> 7.28 us
    sub x3 -> x1, other arithmetic: 5.62 us -> 0.65 us  [adamw(): weight - LEARN_RATE * (update + WEIGHT_DECAY * weight)]
  transfers between devices with their start and end apart: 4 -> 0, of which waited for: 4 -> 0; matrix products, arithmetic and copies ran while one was open for 4% -> 0% of each run, Pallas kernels for 0% -> 0%
where the time goes in v2:
time: 107 us
  Pallas kernels  87.9 us (82%)
  local copies, waits for them, and re-layouts  16.8 us (16%)
  between operations  1.35 us (1%)
    pallas_call x1, Pallas kernels, reduce_grads(): pl.pallas_call(functools.partial(reduce_kernel, replicas, shards), in_spe...  41.2 us
    pallas_call x1, Pallas kernels, gather_weights(): pl.pallas_call(functools.partial(gather_kernel, replicas, shards), in_spe...  24.9 us
    pallas_call x1, Pallas kernels, local_step(): pl.pallas_call(functools.partial(local_kernel, seqs=seqs), grid=(seqs,),...  17 us
    unnamed x17, local copies, waits for them, and re-layouts  7.28 us
    pallas_call x1, Pallas kernels, adam_large(): pl.pallas_call(adam_kernel, in_specs=[pl.BlockSpec(memory_space=pltpu.VME...  4.72 us

profile of v2, /device:TPU:0, one launch (start us, length us, event | category | flops | bytes accessed | tf_op | source)
XLA Modules:
  0.0 106.7 jit_solution(4555714283699370338)
XLA Ops:
  1.3 0.7 slice_bitcast_fusion.1
  2.0 0.6 pad.13.dlog_ref
  2.6 1.3 %slice.28 = f32[256]{0:T(256)} slice(f32[6914]{0:T(1024)} %param.17), slice={[6658:6914]} | slice | bytes 2048 | tf_op jit(solution)/shard_map/slice | solution.py:40
  3.9 1.3 %slice.24 = f32[512]{0:T(512)} slice(f32[6914]{0:T(1024)} %param.17), slice={[0:512]} | slice | bytes 4096 | tf_op jit(solution)/shard_map/slice | solution.py:36
  5.2 0.7 slice.25
  5.9 0.7 slice.26
  6.6 0.6 reshape.54.taps_ref
  7.2 0.3 reshape.53
  7.5 0.7 pad.12.bw_ref
  8.2 0.0 copy-start.2
  8.2 1.1 %copy-done.2 = f32[128,1536]{1,0:T(8,128)S(1)} copy-done((f32[128,1536]{1,0:T(8,128)S(1)}, f32[128,1536]{1,0:T(8,128)}, u32[]{:S(2)}) %copy-start.2) | copy-done | bytes 786456
  9.3 0.0 copy-start.3
  9.3 0.9 copy-done.3
  10.3 24.9 %gather_weights.1 = bf16[4,2048,128]{2,1,0:T(8,128)(2,1)S(1)} custom-call(f32[128,1536]{1,0:T(8,128)S(1)} %copy-done.2, f32[128,512]{1,0:T(8,128)S(1)} %copy-done.3), custom_call_target="tpu_custom_call" | custom-call | tf_op jit(solution)/shard_map/gather_weights/pallas_call | solution.py:568
  35.2 0.0 copy-start
  35.2 1.3 %copy-done = bf16[4,2048,128]{2,1,0:T(8,128)(2,1)} copy-done((bf16[4,2048,128]{2,1,0:T(8,128)(2,1)}, bf16[4,2048,128]{2,1,0:T(8,128)(2,1)S(1)}, u32[]{:S(2)}) %copy-start) | copy-done | bytes 2097176
  36.5 0.0 copy-start.5
  36.5 0.0 copy-start.6
  36.5 0.0 copy-start.7
  36.5 17.0 %local_step.1 = (f32[1,256,512]{2,1,0:T(8,128)}, f32[1,256,512]{2,1,0:T(8,128)}, f32[4,16,128,128]{3,2,1,0:T(8,128)}, f32[1,512]{1,0:T(1,128)}, f32[512,128]{1,0...) custom-call(s32[1]{0:T(128)S(6)} %copy.29.flag_ref, bf16[1,256,512]{2,1,0:T(8,128)(2,1)} %x_ref.1, ...), custom_call_target="tpu_custom_call" | custom-call | tf_op jit(solution)/shard_map/local_step/pallas_call | solution.py:435
  53.6 0.7 slice_bitcast_fusion
  54.3 1.1 %reshape.56 = f32[2048]{0:T(1024)S(1)} reshape(f32[512,4]{1,0:T(8,128)} %bitcast.21) | data formatting | bytes 16384 | tf_op jit(solution)/shard_map/reshape | solution.py:782
  55.4 0.7 copy.28
  56.1 0.8 concatenate.3
  56.9 0.0 copy-start.1
  56.9 2.2 %copy-done.1 = f32[4,16,128,128]{3,2,1,0:T(8,128)S(1)} copy-done((f32[4,16,128,128]{3,2,1,0:T(8,128)S(1)}, f32[4,16,128,128]{3,2,1,0:T(8,128)}, u32[]{:S(2)}) %copy-start.1) | copy-done | bytes 4194328
  59.1 41.2 %reduce_grads.1 = (f32[2048,128]{1,0:T(8,128)S(1)}, f32[64,128]{1,0:T(8,128)S(1)}) custom-call(f32[4,2048,128]{2,1,0:T(8,128)S(1)} %bitcast.19, f32[1,64,128]{2,1,0:T(8,128)S(1)} %pad_bitcast_fusion.small_ref), custom_call_target="tpu_custom_call" | custom-call | tf_op jit(solution)/shard_map/reduce_grads/pallas_call | solution.py:685
  100.3 0.0 copy-start.4
  100.3 1.0 copy-done.4
  101.3 0.0 copy-done.5
  101.3 0.0 copy-done.6
  101.3 0.0 copy-done.7
  101.3 0.6 multiply_subtract_fusion
  101.9 4.7 %adam_large.1 = (f32[128,1536]{1,0:T(8,128)}, f32[128,1536]{1,0:T(8,128)}, f32[128,1536]{1,0:T(8,128)}, f32[128,1536]{1,0:T(8,128)}, f32[128,512]{1,0:T(8,128)},...) custom-call(f32[2048,128]{1,0:T(8,128)} %copy-done.4, f32[128,1536]{1,0:T(8,128)} %refs_0_.1, ...), custom_call_target="tpu_custom_call" | custom-call | tf_op jit(solution)/shard_map/adam_large/pallas_call | solution.py:719
  (1 shorter events, 0.0 us)
Async XLA Ops:
  8.2 1.1 %copy-start.2 = (f32[128,1536]{1,0:T(8,128)S(1)}, f32[128,1536]{1,0:T(8,128)}, u32[]{:S(2)}) copy-start(f32[128,1536]{1,0:T(8,128)} %refs_0_.1) | copy-start | bytes 2359300
  9.3 0.9 copy-start.3
  35.2 1.3 %copy-start = (bf16[4,2048,128]{2,1,0:T(8,128)(2,1)}, bf16[4,2048,128]{2,1,0:T(8,128)(2,1)S(1)}, u32[]{:S(2)}) copy-start(bf16[4,2048,128]{2,1,0:T(8,128)(2,1)S(1)} %gather_weights.1) | copy-start | bytes 6291460
  36.5 64.8 %copy-start.5 = (f32[6914]{0:T(1024)S(1)}, f32[6914]{0:T(1024)}, u32[]{:S(2)}) copy-start(f32[6914]{0:T(1024)} %param.17) | copy-start | bytes 82972
  36.5 64.8 %copy-start.6 = (f32[6914]{0:T(1024)S(1)}, f32[6914]{0:T(1024)}, u32[]{:S(2)}) copy-start(f32[6914]{0:T(1024)} %param.22) | copy-start | bytes 82972
  36.5 64.8 %copy-start.7 = (f32[6914]{0:T(1024)S(1)}, f32[6914]{0:T(1024)}, u32[]{:S(2)}) copy-start(f32[6914]{0:T(1024)} %param.23) | copy-start | bytes 82972
  56.9 2.2 %copy-start.1 = (f32[4,16,128,128]{3,2,1,0:T(8,128)S(1)}, f32[4,16,128,128]{3,2,1,0:T(8,128)}, u32[]{:S(2)}) copy-start(f32[4,16,128,128]{3,2,1,0:T(8,128)} %get-tuple-element.34) | copy-start | bytes 12582916
  100.3 1.0 copy-start.4

commit v3 on v2

--- a/solution.py
+++ b/solution.py
@@ -13,7 +13,8 @@
 DV = 256
 CONV = 4
 CHUNK = 128
-GROUPS = 4
+GATHER_GROUPS = 4
+REDUCE_GROUPS = 8
 MESH = pl.DeviceIdType.MESH
 STEP = 3
 
@@ -482,9 +483,16 @@
     return rep + (1 << bit) * (1 - 2 * bit_of(rep, bit))
 
 
-def bit_orders(replicas):
+def bit_orders(replicas, groups):
     bits = list(range(replicas.bit_length() - 1))
-    return [bits, bits[:1] + bits[1:][::-1]]
+    orders = (bits, bits[:1] + bits[1:][::-1])
+    return [orders[g % 2] for g in range(groups)]
+
+
+def group_count(rows, replicas, tile, most):
+    while most > 1 and rows % (most * replicas * tile):
+        most //= 2
+    return most
 
 
 def aligned(offset, size):
@@ -526,8 +534,9 @@
     full_ref[shard] = mine_ref[...]
     greet(replicas, shards)
     copies = Copies(send_sems, recv_sems)
-    orders = bit_orders(replicas)
-    span = mine_ref.shape[0] // len(orders)
+    total_rows = mine_ref.shape[0]
+    orders = bit_orders(replicas, group_count(total_rows, replicas, 16, GATHER_GROUPS))
+    span = total_rows // len(orders)
     state = []
     for g, order in enumerate(orders):
         size, base = span, g * span
@@ -564,7 +573,8 @@
     rows, block = in_weight.shape[0], 128
     total_rows = rows * (in_weight.shape[1] + out_weight.shape[1]) // block
     bits = replicas.bit_length() - 1
-    count = 2 * (bits + shards - 1)
+    groups = group_count(total_rows, replicas, 16, GATHER_GROUPS)
+    count = groups * (bits + shards - 1)
     return pl.pallas_call(
         functools.partial(gather_kernel, replicas, shards),
         in_specs=[pl.BlockSpec(memory_space=pltpu.VMEM)] * 2,
@@ -585,16 +595,17 @@
 def reduce_kernel(replicas, shards, grad_ref, small_ref, out_ref, small_out_ref, *scratch):
     rep, shard = lax.axis_index("rep"), lax.axis_index("fsdp")
     send_sems, recv_sems = scratch[-2:]
-    orders = bit_orders(replicas)
+    count = group_count(grad_ref.shape[1], replicas, 8, REDUCE_GROUPS)
+    orders = bit_orders(replicas, count + 1)
     bits = len(orders[0])
     copies = Copies(send_sems, recv_sems)
     greet(replicas, shards)
-    span = grad_ref.shape[1] // GROUPS
+    span = grad_ref.shape[1] // count
     groups = []
-    for g in range(GROUPS + 1):
+    for g in range(count + 1):
         bufs = scratch[g * (bits + 1) : (g + 1) * (bits + 1)]
-        if g < GROUPS:
-            groups.append([grad_ref, out_ref, g * span, span, orders[g % 2], bufs])
+        if g < count:
+            groups.append([grad_ref, out_ref, g * span, span, orders[g], bufs])
         else:
             groups.append(
                 [small_ref, small_out_ref, 0, small_ref.shape[1], orders[0], bufs]
@@ -624,7 +635,7 @@
                 pending = []
                 for step in range(1, shards):
                     to = lax.rem(shard + step, shards)
-                    if g < GROUPS:
+                    if g < count:
                         src, slot = group[0].at[to], bufs[bits].at[step - 1]
                     else:
                         src, slot = group[0].at[0], bufs[bits].at[shard]
@@ -633,16 +644,16 @@
     spread = []
     for g, group in enumerate(groups):
         cur, out, _, size, order, bufs = group
-        base = g * span if g < GROUPS else 0
-        full = span if g < GROUPS else small_ref.shape[1]
+        base = g * span if g < count else 0
+        full = span if g < count else small_ref.shape[1]
         for bit in order:
             full //= 2
             base = base + bit_of(rep, bit) * full
-        if g == GROUPS:
+        if g == count:
             bufs[bits][shard] = cur[0]
         for copy in live[g]:
             copy.wait_recv()
-        if g < GROUPS:
+        if g < count:
             value = cur[shard]
             for step in range(1, shards):
                 value = value + bufs[bits][step - 1]
@@ -673,15 +684,16 @@
 def reduce_grads(replicas, shards, grads, small):
     rows, block = grads.shape[1:]
     bits = replicas.bit_length() - 1
+    groups = group_count(rows, replicas, 8, REDUCE_GROUPS)
     scratch = []
-    for g in range(GROUPS + 1):
-        parts, size = (shards, rows // GROUPS) if g < GROUPS else (1, small.shape[1])
+    for g in range(groups + 1):
+        parts, size = (shards, rows // groups) if g < groups else (1, small.shape[1])
         for _ in range(bits):
             size //= 2
             scratch.append(pltpu.VMEM((parts, size, block), jnp.float32))
-        slots = shards - 1 if g < GROUPS else shards
+        slots = shards - 1 if g < groups else shards
         scratch.append(pltpu.VMEM((slots, size, block), jnp.float32))
-    count = (GROUPS + 1) * (2 * bits + shards - 1)
+    count = (groups + 1) * (2 * bits + shards - 1)
     return pl.pallas_call(
         functools.partial(reduce_kernel, replicas, shards),
         in_specs=[pl.BlockSpec(memory_space=pltpu.VMEM)] * 2,

time: 107 us -> 104 us (0.972)
  Pallas kernels: 87.9 us -> 84.6 us
    pallas_call x1, Pallas kernels: 24.9 us -> 22.8 us  [gather_weights(): pl.pallas_call(functools.partial(gather_kernel, replicas, shards), in_spe...]
    pallas_call x1, Pallas kernels: 41.2 us -> 40.1 us  [reduce_grads(): pl.pallas_call(functools.partial(reduce_kernel, replicas, shards), in_spe...]
where the time goes in v3:
time: 104 us; the launch traced here: 103 us
  Pallas kernels  84.6 us (81%)
  local copies, waits for them, and re-layouts  16.8 us (16%)
  between operations  1.35 us (1%)
    pallas_call x1, Pallas kernels, reduce_grads(): pl.pallas_call(functools.partial(reduce_kernel, replicas, shards), in_spe...  40.1 us
    pallas_call x1, Pallas kernels, gather_weights(): pl.pallas_call(functools.partial(gather_kernel, replicas, shards), in_spe...  22.8 us
    pallas_call x1, Pallas kernels, local_step(): pl.pallas_call(functools.partial(local_kernel, seqs=seqs), grid=(seqs,),...  17 us
    unnamed x17, local copies, waits for them, and re-layouts  7.28 us
    pallas_call x1, Pallas kernels, adam_large(): pl.pallas_call(adam_kernel, in_specs=[pl.BlockSpec(memory_space=pltpu.VME...  4.72 us

profile of v3, /device:TPU:0, one launch (start us, length us, event | category | flops | bytes accessed | tf_op | source)
XLA Modules:
  0.0 103.4 jit_solution(10615714254285940931)
XLA Ops:
  1.3 0.7 slice_bitcast_fusion.1
  2.0 0.6 pad.13.dlog_ref
  2.6 1.3 %slice.28 = f32[256]{0:T(256)} slice(f32[6914]{0:T(1024)} %param.17), slice={[6658:6914]} | slice | bytes 2048 | tf_op jit(solution)/shard_map/slice | solution.py:41
  3.9 1.3 %slice.24 = f32[512]{0:T(512)} slice(f32[6914]{0:T(1024)} %param.17), slice={[0:512]} | slice | bytes 4096 | tf_op jit(solution)/shard_map/slice | solution.py:37
  5.2 0.7 slice.25
  5.9 0.7 slice.26
  6.6 0.6 reshape.54.taps_ref
  7.2 0.3 reshape.53
  7.5 0.7 pad.12.bw_ref
  8.2 0.0 copy-start.2
  8.2 1.1 %copy-done.2 = f32[128,1536]{1,0:T(8,128)S(1)} copy-done((f32[128,1536]{1,0:T(8,128)S(1)}, f32[128,1536]{1,0:T(8,128)}, u32[]{:S(2)}) %copy-start.2) | copy-done | bytes 786456
  9.3 0.0 copy-start.3
  9.3 0.9 copy-done.3
  10.3 22.8 %gather_weights.1 = bf16[4,2048,128]{2,1,0:T(8,128)(2,1)S(1)} custom-call(f32[128,1536]{1,0:T(8,128)S(1)} %copy-done.2, f32[128,512]{1,0:T(8,128)S(1)} %copy-done.3), custom_call_target="tpu_custom_call" | custom-call | tf_op jit(solution)/shard_map/gather_weights/pallas_call | solution.py:578
  33.0 0.0 copy-start
  33.1 1.3 %copy-done = bf16[4,2048,128]{2,1,0:T(8,128)(2,1)} copy-done((bf16[4,2048,128]{2,1,0:T(8,128)(2,1)}, bf16[4,2048,128]{2,1,0:T(8,128)(2,1)S(1)}, u32[]{:S(2)}) %copy-start) | copy-done | bytes 2097176
  34.4 0.0 copy-start.5
  34.4 0.0 copy-start.6
  34.4 0.0 copy-start.7
  34.4 17.0 %local_step.1 = (f32[1,256,512]{2,1,0:T(8,128)}, f32[1,256,512]{2,1,0:T(8,128)}, f32[4,16,128,128]{3,2,1,0:T(8,128)}, f32[1,512]{1,0:T(1,128)}, f32[512,128]{1,0...) custom-call(s32[1]{0:T(128)S(6)} %copy.29.flag_ref, bf16[1,256,512]{2,1,0:T(8,128)(2,1)} %x_ref.1, ...), custom_call_target="tpu_custom_call" | custom-call | tf_op jit(solution)/shard_map/local_step/pallas_call | solution.py:436
  51.4 0.7 slice_bitcast_fusion
  52.1 1.1 %reshape.56 = f32[2048]{0:T(1024)S(1)} reshape(f32[512,4]{1,0:T(8,128)} %bitcast.21) | data formatting | bytes 16384 | tf_op jit(solution)/shard_map/reshape | solution.py:794
  53.2 0.7 copy.28
  54.0 0.8 concatenate.3
  54.7 0.0 copy-start.1
  54.7 2.2 %copy-done.1 = f32[4,16,128,128]{3,2,1,0:T(8,128)S(1)} copy-done((f32[4,16,128,128]{3,2,1,0:T(8,128)S(1)}, f32[4,16,128,128]{3,2,1,0:T(8,128)}, u32[]{:S(2)}) %copy-start.1) | copy-done | bytes 4194328
  56.9 40.1 %reduce_grads.1 = (f32[2048,128]{1,0:T(8,128)S(1)}, f32[64,128]{1,0:T(8,128)S(1)}) custom-call(f32[4,2048,128]{2,1,0:T(8,128)S(1)} %bitcast.19, f32[1,64,128]{2,1,0:T(8,128)S(1)} %pad_bitcast_fusion.small_ref), custom_call_target="tpu_custom_call" | custom-call | tf_op jit(solution)/shard_map/reduce_grads/pallas_call | solution.py:697
  97.0 0.0 copy-start.4
  97.0 1.0 copy-done.4
  98.0 0.0 copy-done.5
  98.0 0.0 copy-done.6
  98.0 0.0 copy-done.7
  98.0 0.6 multiply_subtract_fusion
  98.6 4.7 %adam_large.1 = (f32[128,1536]{1,0:T(8,128)}, f32[128,1536]{1,0:T(8,128)}, f32[128,1536]{1,0:T(8,128)}, f32[128,1536]{1,0:T(8,128)}, f32[128,512]{1,0:T(8,128)},...) custom-call(f32[2048,128]{1,0:T(8,128)} %copy-done.4, f32[128,1536]{1,0:T(8,128)} %refs_0_.1, ...), custom_call_target="tpu_custom_call" | custom-call | tf_op jit(solution)/shard_map/adam_large/pallas_call | solution.py:731
  (1 shorter events, 0.0 us)
Async XLA Ops:
  8.2 1.1 %copy-start.2 = (f32[128,1536]{1,0:T(8,128)S(1)}, f32[128,1536]{1,0:T(8,128)}, u32[]{:S(2)}) copy-start(f32[128,1536]{1,0:T(8,128)} %refs_0_.1) | copy-start | bytes 2359300
  9.3 0.9 copy-start.3
  33.0 1.3 %copy-start = (bf16[4,2048,128]{2,1,0:T(8,128)(2,1)}, bf16[4,2048,128]{2,1,0:T(8,128)(2,1)S(1)}, u32[]{:S(2)}) copy-start(bf16[4,2048,128]{2,1,0:T(8,128)(2,1)S(1)} %gather_weights.1) | copy-start | bytes 6291460
  34.4 63.6 %copy-start.5 = (f32[6914]{0:T(1024)S(1)}, f32[6914]{0:T(1024)}, u32[]{:S(2)}) copy-start(f32[6914]{0:T(1024)} %param.17) | copy-start | bytes 82972
  34.4 63.6 %copy-start.6 = (f32[6914]{0:T(1024)S(1)}, f32[6914]{0:T(1024)}, u32[]{:S(2)}) copy-start(f32[6914]{0:T(1024)} %param.22) | copy-start | bytes 82972
  34.4 63.6 %copy-start.7 = (f32[6914]{0:T(1024)S(1)}, f32[6914]{0:T(1024)}, u32[]{:S(2)}) copy-start(f32[6914]{0:T(1024)} %param.23) | copy-start | bytes 82972
  54.7 2.2 %copy-start.1 = (f32[4,16,128,128]{3,2,1,0:T(8,128)S(1)}, f32[4,16,128,128]{3,2,1,0:T(8,128)}, u32[]{:S(2)}) copy-start(f32[4,16,128,128]{3,2,1,0:T(8,128)} %get-tuple-element.34) | copy-start | bytes 12582916
  97.0 1.0 copy-start.4
